TPU v7x, 512 devices: a whole 4x4x16 slice. The times are simulated.
512 devices in a mesh: ctx: 128 (over z, x, core), tp: 4 (over y).
Axes of the slice: x: 4, y: 4, z: 16, core: 2. Of those that a mesh axis runs over, the one named last changes fastest.
Arguments:
- projected: bfloat16 [16384, 3, 4096], P('ctx', None, 'tp'), may hold values from -6 to 6
- short_taps: float32 [3, 7, 4096], P(None, None, 'tp'), may hold values from -2 to 2
- residues: float32 [4096, 16], P('tp'), may hold values from -6 to 6
- rates: float32 [4096, 16], P('tp'), may hold values from 0.3 to 1024
- skip_gain: float32 [4096], P('tp'), may hold values from -1 to 1
- norm_gain: float32 [4096], P('tp'), may hold values from 0.5 to 1.5
Outputs:
- mixed_out: bfloat16 [16384, 4096], P('ctx', 'tp')
All inputs are finite; a program needn't handle non-finite values.
Results may differ from a plain program's by a relative error of at most 0.008.
Values may be sent and summed in bfloat16 or wider, within the bound.
No kernel may reach another device: no remote copies, remote signals or barrier semaphores. Data moves between devices by JAX's collectives and lax.ppermute only.
A program may use at most 64 MiB of HBM per device.

v0:
```python
import math

import jax
import jax.numpy as jnp
from jax import lax
from jax.experimental import pallas as pl
from jax.experimental.pallas import tpu as pltpu
from jax.sharding import PartitionSpec as P

TAPS = 7
MODES = 16
LANES = 128
SUB = 8
PLANE = 8
RIM = 8
HIGHEST = lax.Precision.HIGHEST
F32 = jnp.float32


def whole(memory_space=pltpu.VMEM):
    return pl.BlockSpec(memory_space=memory_space)


def spread(dst, base, src, rows):
    for j in range(SUB):
        dst[pl.ds(base * SUB + j, rows, stride=SUB), :] = src[:, j * LANES : (j + 1) * LANES]


def local_kernel(
    length, proj, rim, taps, rates, residues, skip, state_out, base_out, query_out, xs, tap_s, mode_s
):
    rows = proj.shape[1]
    for g in range(3):
        spread(xs.at[g], 0, rim[g].astype(F32), RIM)
        spread(xs.at[g], RIM, proj[g].astype(F32), rows)
        spread(tap_s.at[g], 0, taps[g], TAPS)
    spread(mode_s.at[0], 0, jnp.exp(rates[...] * (-1.0 / length)), MODES)
    spread(mode_s.at[1], 0, residues[...] * (1.0 / math.sqrt(length)), MODES)

    def tile(ref, row):
        return ref[pl.ds(pl.multiple_of(row * SUB, SUB), SUB), :]

    group = 8

    def conv_step(step, carry):
        first = step * group
        done = []
        for g in range(3):
            window = [tile(xs.at[g], first + RIM - (TAPS - 1) + i) for i in range(group + TAPS - 1)]
            weights = [tile(tap_s.at[g], j) for j in range(TAPS)]
            outs = []
            for i in range(group):
                total = weights[0] * window[i + TAPS - 1]
                for j in range(1, TAPS):
                    total = total + weights[j] * window[i + TAPS - 1 - j]
                outs.append(total)
            done.append(outs)
        for i in range(group):
            query_out[first + i] = done[0][i]
            base_out[first + i] = (
                (done[1][i] * done[2][i]).astype(jnp.bfloat16).astype(F32)
            )
        return carry

    lax.fori_loop(0, rows // group, conv_step, 0)

    decay = [tile(mode_s.at[0], n) for n in range(MODES)]
    weight = [tile(mode_s.at[1], n) for n in range(MODES)]
    direct = skip[...]

    def scan_step(step, state):
        first = step * 4
        state = list(state)
        for i in range(4):
            kv = base_out[first + i]
            total = direct * kv
            for n in range(MODES):
                state[n] = decay[n] * state[n] + kv
            parts = [weight[n] * state[n] for n in range(MODES)]
            while len(parts) > 1:
                parts = [parts[k] + parts[k + 1] for k in range(0, len(parts), 2)]
            base_out[first + i] = total + parts[0]
        return tuple(state)

    zero = jnp.zeros((SUB, LANES), F32)
    state = lax.fori_loop(0, rows // 4, scan_step, (zero,) * MODES)
    for n in range(MODES):
        state_out[pl.ds(n, SUB, stride=MODES), :] = state[n]


def total_kernel(block, length, planes, states, rates, total_out):
    step = jnp.exp(rates[...] * (-float(block) / length))
    total = states[0]
    for p in range(1, PLANE):
        total = step * total + states[p]
    total = total.astype(total_out.dtype)
    for z in range(planes):
        total_out[z] = total


def carry_kernel(block, length, planes, where, totals, states, rates, carry_out):
    mine = where[0]
    rate = rates[...]
    carry = jnp.zeros((MODES, LANES), F32)
    for z in range(planes):
        gap = jnp.maximum(mine - 1 - z, 0).astype(F32) * (float(block * PLANE) / length)
        share = jnp.exp(-(rate * gap)) * totals[z].astype(F32)
        carry = carry + jnp.where(z < mine, share, 0.0)
    step = jnp.exp(rate * (-float(block) / length))
    for p in range(PLANE):
        carry_out[p] = carry
        carry = step * carry + states[p]


def gate_kernel(
    length, carry, rates, residues, base, query, gated_out, squares_out, mode_s, tiles
):
    rows = base.shape[0]
    spread(mode_s.at[0], 0, jnp.exp(rates[...] * (-1.0 / length)), MODES)
    spread(mode_s.at[1], 0, residues[...] * (1.0 / math.sqrt(length)), MODES)

    def tile(ref, row):
        return ref[pl.ds(pl.multiple_of(row * SUB, SUB), SUB), :]

    decay = [tile(mode_s.at[0], n) for n in range(MODES)]
    start = tuple(
        decay[n] * tile(mode_s.at[1], n) * carry[pl.ds(n, SUB, stride=MODES), :]
        for n in range(MODES)
    )

    def step_fn(step, state):
        first = step * 4
        state = list(state)
        for i in range(4):
            parts = list(state)
            while len(parts) > 1:
                parts = [parts[k] + parts[k + 1] for k in range(0, len(parts), 2)]
            value = query[first + i] * (base[first + i] + parts[0])
            tiles[pl.ds(pl.multiple_of((first + i) * SUB, SUB), SUB), :] = value
            state = [decay[n] * state[n] for n in range(MODES)]
        return tuple(state)

    lax.fori_loop(0, rows // 4, step_fn, start)
    squares = jnp.zeros((rows, LANES), F32)
    for j in range(SUB):
        part = tiles[pl.ds(j, rows, stride=SUB), :]
        gated_out[:, j * LANES : (j + 1) * LANES] = part
        squares = squares + part * part
    ones = jnp.ones((SUB, LANES), F32)
    line = lax.dot_general(
        ones, squares, (((1,), (1,)), ((), ())), precision=HIGHEST, preferred_element_type=F32
    )
    squares_out[...] = line[: squares_out.shape[0]]


def norm_kernel(width, gated, squares, gain, out):
    count = squares.shape[0]
    ones = jnp.ones((count, LANES), F32)
    total = lax.dot_general(
        squares[...], ones, (((0,), (0,)), ((), ())), precision=HIGHEST, preferred_element_type=F32
    )
    scale = lax.rsqrt(total * (1.0 / width) + 1e-05)
    for j in range(SUB):
        cols = slice(j * LANES, (j + 1) * LANES)
        out[:, cols] = (gated[:, cols] * gain[:, cols] * scale).astype(out.dtype)


def shards(projected, short_taps, residues, rates, skip_gain, norm_gain):
    rows = projected.shape[0]
    channels = projected.shape[2]
    groups = lax.axis_size("ctx")
    parts = lax.axis_size("tp")
    planes = groups // PLANE
    length = rows * groups
    me = lax.axis_index("ctx")
    in_plane = [[z * PLANE + p for p in range(PLANE)] for z in range(planes)]
    along_z = [[z * PLANE + p for z in range(planes)] for p in range(PLANE)]

    proj = jnp.transpose(projected, (1, 0, 2))
    rate_t = rates.T
    residue_t = residues.T
    rim = lax.ppermute(
        proj[:, rows - RIM :], "ctx", [(i, i + 1) for i in range(groups - 1)]
    )
    own_rates = lax.dynamic_slice_in_dim(rate_t, (me % PLANE) * LANES, LANES, 1)
    plane_at = (me // PLANE).astype(jnp.int32).reshape(1)

    states, base, query = pl.pallas_call(
        lambda *refs: local_kernel(length, *refs),
        name="local",
        out_shape=(
            jax.ShapeDtypeStruct((SUB * MODES, LANES), F32),
            jax.ShapeDtypeStruct((rows, SUB, LANES), F32),
            jax.ShapeDtypeStruct((rows, SUB, LANES), F32),
        ),
        in_specs=[whole()] * 6,
        out_specs=(whole(),) * 3,
        scratch_shapes=[
            pltpu.VMEM((3, (RIM + rows) * SUB, LANES), F32),
            pltpu.VMEM((3, TAPS * SUB, LANES), F32),
            pltpu.VMEM((2, MODES * SUB, LANES), F32),
        ],
        compiler_params=pltpu.CompilerParams(vmem_limit_bytes=32 << 20),
    )(proj, rim, short_taps, rate_t, residue_t, skip_gain.reshape(SUB, LANES))

    met = lax.all_to_all(
        states.reshape(SUB, MODES, LANES), "ctx", 0, 0, tiled=True, axis_index_groups=in_plane
    )
    totals = pl.pallas_call(
        lambda *refs: total_kernel(rows, length, planes, *refs),
        name="total",
        out_shape=jax.ShapeDtypeStruct((planes, MODES, LANES), jnp.bfloat16),
        in_specs=[whole()] * 2,
        out_specs=whole(),
    )(met, own_rates)
    gathered = lax.all_to_all(totals, "ctx", 0, 0, tiled=True, axis_index_groups=along_z)
    carries = pl.pallas_call(
        lambda *refs: carry_kernel(rows, length, planes, *refs),
        name="carry",
        out_shape=jax.ShapeDtypeStruct((PLANE, MODES, LANES), F32),
        in_specs=[whole(pltpu.SMEM)] + [whole()] * 3,
        out_specs=whole(),
    )(plane_at, gathered, met, own_rates)
    carry = lax.all_to_all(carries, "ctx", 0, 0, tiled=True, axis_index_groups=in_plane)

    gated, squares = pl.pallas_call(
        lambda *refs: gate_kernel(length, *refs),
        name="gate",
        out_shape=(
            jax.ShapeDtypeStruct((rows, channels), F32),
            jax.ShapeDtypeStruct((parts, rows), F32),
        ),
        in_specs=[whole()] * 5,
        out_specs=(whole(),) * 2,
        scratch_shapes=[
            pltpu.VMEM((2, MODES * SUB, LANES), F32),
            pltpu.VMEM((rows * SUB, LANES), F32),
        ],
        compiler_params=pltpu.CompilerParams(vmem_limit_bytes=32 << 20),
    )(carry.reshape(SUB * MODES, LANES), rate_t, residue_t, base, query)
    squares = lax.all_to_all(squares, "tp", 0, 0, tiled=True)
    return pl.pallas_call(
        lambda *refs: norm_kernel(channels * parts, *refs),
        name="norm",
        out_shape=jax.ShapeDtypeStruct((rows, channels), jnp.bfloat16),
        in_specs=[whole()] * 3,
        out_specs=whole(),
    )(gated, squares, norm_gain.reshape(1, channels))


def solution(mesh):
    return jax.shard_map(
        shards,
        mesh=mesh,
        in_specs=(
            P("ctx", None, "tp"),
            P(None, None, "tp"),
            P("tp", None),
            P("tp", None),
            P("tp"),
            P("tp"),
        ),
        out_specs=P("ctx", "tp"),
        check_vma=False,
    )
```

profile of v0, /device:TPU:1, one launch (start us, length us, event | category | flops | bytes accessed | tf_op | source)
XLA Modules:
  0.0 77.7 jit_solution(16929925332663283814)
XLA Ops:
  0.0 0.8 %slice.4 = bf16[3,8,1024]{2,1,0:T(8,128)(2,1)S(1)} slice(bf16[3,128,1024]{2,1,0:T(8,128)(2,1)} %bitcast.14), slice={[0:3], [120:128], [0:1024]} | slice | bytes 98304 | tf_op jit(solution)/shard_map/slice | solution.py:183
  0.8 4.5 %collective-permute-start = (bf16[3,8,1024]{2,1,0:T(8,128)(2,1)S(1)}, bf16[3,8,1024]{2,1,0:T(8,128)(2,1)S(1)}, u32[]{:S(2)}, u32[]{:S(2)}) collective-permute-start(bf16[3,8,1024]{2,1,0:T(8,128)(2,1)S(1)} %slice.4), channel_id=1, source_target_pairs={{0,4},{4,8},{8,12},{12,16},{16,20},{20,24},{24,28},{28,32},{32,36}... | collective-permute-start | bytes 147464 | tf_op jit(solution)/shard_map/ppermute | solution.py:182
  5.4 0.0 copy-start.5
  5.4 4.3 %collective-permute-done.refs_1_ = bf16[3,8,1024]{2,1,0:T(8,128)(2,1)S(1)} collective-permute-done((bf16[3,8,1024]{2,1,0:T(8,128)(2,1)S(1)}, bf16[3,8,1024]{2,1,0:T(8,128)(2,1)S(1)}, u32[]{:S(2)}, u32[]{:S(2)}) %collective-permute-start) | collective-permute-done | bytes 49184 | tf_op jit(solution)/shard_map/ppermute | solution.py:182
  9.7 0.0 copy-done.2
  9.7 0.0 copy-done.3
  9.7 0.0 copy-start
  9.7 1.1 %copy-done = bf16[128,3,1024]{2,0,1:T(8,128)(2,1)S(1)} copy-done((bf16[128,3,1024]{2,0,1:T(8,128)(2,1)S(1)}, bf16[128,3,1024]{2,0,1:T(8,128)(2,1)}, u32[]{:S(2)}) %copy-start) | copy-done | bytes 786456
  10.9 0.9 %copy-done.4 = f32[3,7,1024]{2,1,0:T(8,128)S(1)} copy-done((f32[3,7,1024]{2,1,0:T(8,128)S(1)}, f32[3,7,1024]{2,1,0:T(8,128)}, u32[]{:S(2)}) %copy-start.4) | copy-done | bytes 86040
  11.8 3.3 %local.1 = (f32[128,128]{1,0:T(8,128)}, f32[128,8,128]{2,1,0:T(8,128)S(1)}, f32[128,8,128]{2,1,0:T(8,128)S(1)}) custom-call(bf16[3,128,1024]{2,1,0:T(8,128)(2,1)S(1)} %bitcast.15, bf16[3,8,1024]{2,1,0:T(8,128)(2,1)S(1)} %collective-permute-done.refs_1_, f32[3,7,1024]{2,1,0:T(8,128)S(1)} %copy-done.4, f32[16,1024]{1,0:T(8,128)S(1)} %bitcast.16, ...), custom_call_target="tpu_custom_call" | custom-call | tf_op jit(solution)/shard_map/local/pallas_call | solution.py:188
  15.1 3.4 %all-to-all-start = ((f32[8,16,128]{2,1,0:T(8,128)}), f32[8,16,128]{2,1,0:T(8,128)S(1)}, u32[]{:S(2)}, u32[]{:S(2)}) async-start(f32[8,16,128]{2,1,0:T(8,128)} %bitcast.5), calls=%async_computation | async-start | bytes 131072 | tf_op jit(solution)/shard_map/all_to_all | solution.py:206
  18.5 0.6 dynamic-slice_bitcast_fusion.refs_1_.refs_3_
  19.1 4.3 %all-to-all-done.refs_0_.refs_2_ = f32[8,16,128]{2,1,0:T(8,128)S(1)} async-done(((f32[8,16,128]{2,1,0:T(8,128)}), f32[8,16,128]{2,1,0:T(8,128)S(1)}, u32[]{:S(2)}, u32[]{:S(2)}) %all-to-all-start) | async-done | bytes 65568 | tf_op jit(solution)/shard_map/all_to_all | solution.py:206
  23.3 0.6 copy-done.6
  24.0 1.5 %total.1 = bf16[16,16,128]{2,1,0:T(8,128)(2,1)} custom-call(f32[8,16,128]{2,1,0:T(8,128)} %copy-done.6, f32[16,128]{1,0:T(8,128)} %dynamic-slice_bitcast_fusion.refs_1_.refs_3_), custom_call_target="tpu_custom_call" | custom-call | tf_op jit(solution)/shard_map/total/pallas_call | solution.py:209
  25.5 16.1 %all-to-all-start.1 = ((bf16[16,16,128]{2,1,0:T(8,128)(2,1)}), bf16[16,16,128]{2,1,0:T(8,128)(2,1)S(1)}, u32[]{:S(2)}, u32[]{:S(2)}) async-start(bf16[16,16,128]{2,1,0:T(8,128)(2,1)} %total.1), calls=%async_computation.1 | async-start | bytes 131072 | tf_op jit(solution)/shard_map/all_to_all | solution.py:216
  41.6 11.6 %all-to-all-done.1.refs_1_ = bf16[16,16,128]{2,1,0:T(8,128)(2,1)S(1)} async-done(((bf16[16,16,128]{2,1,0:T(8,128)(2,1)}), bf16[16,16,128]{2,1,0:T(8,128)(2,1)S(1)}, u32[]{:S(2)}, u32[]{:S(2)}) %all-to-all-start.1) | async-done | bytes 65568 | tf_op jit(solution)/shard_map/all_to_all | solution.py:216
  53.2 0.6 copy-done.7
  53.8 1.6 %carry.1 = f32[8,16,128]{2,1,0:T(8,128)} custom-call(s32[1]{0:T(128)} %bitcast.refs_0_, bf16[16,16,128]{2,1,0:T(8,128)(2,1)} %copy-done.7, f32[8,16,128]{2,1,0:T(8,128)} %copy-done.6, f32[16,128]{1,0:T(8,128)} %dynamic-slice_bitcast_fusion.refs_1_.refs_3_), custom_call_target="tpu_custom_call" | custom-call | tf_op jit(solution)/shard_map/carry/pallas_call | solution.py:217
  55.3 10.3 %all_to_all.26 = f32[8,16,128]{2,1,0:T(8,128)S(1)} all-to-all(f32[8,16,128]{2,1,0:T(8,128)} %carry.1), channel_id=1, replica_groups={{0,4,8,12,16,20,24,28},{32,36,40,44,48,52,56,60},{64,68,72,76,80,84,88,..., dimensions={0} | all-to-all | bytes 131072 | tf_op jit(solution)/shard_map/all_to_all | solution.py:224
  65.7 1.0 %gate.1 = (f32[128,1024]{1,0:T(8,128)S(1)}, f32[4,128]{1,0:T(4,128)S(1)}) custom-call(f32[128,128]{1,0:T(8,128)S(1)} %bitcast.20, f32[16,1024]{1,0:T(8,128)S(1)} %bitcast.17, f32[16,1024]{1,0:T(8,128)S(1)} %bitcast.19, f32[128,8,128]{2,1,0:T(8,128)S(1)} %get-tuple-element.11.refs_3_, f32[128,8,128]{2,1,0:T(8,128)S(1)} %get-tuple-element.12.refs_4_), custom_call_target="tpu_custom_call" | custom-call | tf_op jit(solution)/shard_map/gate/pallas_call | solution.py:226
  66.6 0.8 %copy-done.1 = f32[128,1024]{1,0:T(8,128)} copy-done((f32[128,1024]{1,0:T(8,128)}, f32[128,1024]{1,0:T(8,128)S(1)}, u32[]{:S(2)}) %copy-start.1) | copy-done | bytes 524312
  67.4 8.2 %all_to_all.27 = f32[4,1,128]{2,1,0:T(1,128)} all-to-all(f32[4,1,128]{2,1,0:T(1,128)S(1)} %bitcast.22), channel_id=1, replica_groups=mesh['ctx'=128,'tp'=4] {'tp'}, dimensions={0} | all-to-all | bytes 4096 | tf_op jit(solution)/shard_map/all_to_all | solution.py:241
  75.6 2.1 %norm.1 = bf16[128,1024]{1,0:T(8,128)(2,1)} custom-call(f32[128,1024]{1,0:T(8,128)} %copy-done.1, f32[4,128]{1,0:T(4,128)} %bitcast.23, f32[1,1024]{1,0:T(1,128)} %bitcast.24), custom_call_target="tpu_custom_call" | custom-call | tf_op jit(solution)/shard_map/norm/pallas_call | solution.py:242
  (7 shorter events, 0.0 us)
Async XLA Ops:
  0.0 9.7 %copy-start.2 = (f32[1024,16]{0,1:T(8,128)S(1)}, f32[1024,16]{0,1:T(8,128)}, u32[]{:S(2)}) copy-start(f32[1024,16]{0,1:T(8,128)} %param.9) | copy-start | bytes 196612
  0.0 9.7 %copy-start.3 = (f32[1024,16]{0,1:T(8,128)S(1)}, f32[1024,16]{0,1:T(8,128)}, u32[]{:S(2)}) copy-start(f32[1024,16]{0,1:T(8,128)} %param.8) | copy-start | bytes 196612
  0.8 8.9 %collective-permute-start = (bf16[3,8,1024]{2,1,0:T(8,128)(2,1)S(1)}, bf16[3,8,1024]{2,1,0:T(8,128)(2,1)S(1)}, u32[]{:S(2)}, u32[]{:S(2)}) collective-permute-start(bf16[3,8,1024]{2,1,0:T(8,128)(2,1)S(1)} %slice.4), channel_id=1, source_target_pairs={{0,4},{4,8},{8,12},{12,16},{16,20},{20,24},{24,28},{28,32},{32,36}... | collective-permute-start | bytes 147464 | tf_op jit(solution)/shard_map/ppermute | solution.py:182
  5.4 4.4 %copy-start.5 = (f32[1024]{0:T(1024)S(1)}, f32[1024]{0:T(1024)}, u32[]{:S(2)}) copy-start(f32[1024]{0:T(1024)} %param.10) | copy-start | bytes 12292
  9.7 1.1 %copy-start = (bf16[128,3,1024]{2,0,1:T(8,128)(2,1)S(1)}, bf16[128,3,1024]{2,0,1:T(8,128)(2,1)}, u32[]{:S(2)}) copy-start(bf16[128,3,1024]{2,0,1:T(8,128)(2,1)} %param.6) | copy-start | bytes 2359300
  10.9 0.9 %copy-start.4 = (f32[3,7,1024]{2,1,0:T(8,128)S(1)}, f32[3,7,1024]{2,1,0:T(8,128)}, u32[]{:S(2)}) copy-start(f32[3,7,1024]{2,1,0:T(8,128)} %refs_2_.1) | copy-start | bytes 258052
  15.1 8.3 %all-to-all-start = ((f32[8,16,128]{2,1,0:T(8,128)}), f32[8,16,128]{2,1,0:T(8,128)S(1)}, u32[]{:S(2)}, u32[]{:S(2)}) async-start(f32[8,16,128]{2,1,0:T(8,128)} %bitcast.5), calls=%async_computation | async-start | bytes 131072 | tf_op jit(solution)/shard_map/all_to_all | solution.py:206
  23.3 0.6 copy-start.6
  25.5 27.7 %all-to-all-start.1 = ((bf16[16,16,128]{2,1,0:T(8,128)(2,1)}), bf16[16,16,128]{2,1,0:T(8,128)(2,1)S(1)}, u32[]{:S(2)}, u32[]{:S(2)}) async-start(bf16[16,16,128]{2,1,0:T(8,128)(2,1)} %total.1), calls=%async_computation.1 | async-start | bytes 131072 | tf_op jit(solution)/shard_map/all_to_all | solution.py:216
  53.2 0.6 copy-start.7
  66.6 0.8 %copy-start.1 = (f32[128,1024]{1,0:T(8,128)}, f32[128,1024]{1,0:T(8,128)S(1)}, u32[]{:S(2)}) copy-start(f32[128,1024]{1,0:T(8,128)S(1)} %get-tuple-element.13.refs_0_) | copy-start | bytes 1572868
where the time goes:
time: 78.3 us; the launch traced here: 77.7 us
  starting transfers between devices  24 us (31%)
  waiting for transfers between devices  20.2 us (26%)
  blocking collectives  18.5 us (24%)
  Pallas kernels  9.39 us (12%)
  local copies, waits for them, and re-layouts  5.54 us (7%)
    all_to_all x1, starting transfers between devices, shards(): lax.all_to_all(totals, 'ctx', 0, 0, tiled=True, axis_index_groups=along_z)  16.1 us
    all_to_all x1, waiting for transfers between devices, shards(): lax.all_to_all(totals, 'ctx', 0, 0, tiled=True, axis_index_groups=along_z)  11.6 us
    all_to_all x1, blocking collectives, shards(): lax.all_to_all(carries, 'ctx', 0, 0, tiled=True, axis_index_groups=in_plane)  10.3 us
    all_to_all x1, blocking collectives, shards(): squares = lax.all_to_all(squares, 'tp', 0, 0, tiled=True)  8.18 us
    ppermute x1, starting transfers between devices, shards(): lax.ppermute(proj[:, rows - RIM:], 'ctx', [(i, i + 1) for i in range(grou...  4.5 us
    ppermute x1, waiting for transfers between devices, shards(): lax.ppermute(proj[:, rows - RIM:], 'ctx', [(i, i + 1) for i in range(grou...  4.33 us
    all_to_all x1, waiting for transfers between devices, shards(): lax.all_to_all(states.reshape(SUB, MODES, LANES), 'ctx', 0, 0, tiled=True...  4.27 us
    unnamed x16, local copies, waits for them, and re-layouts  4.1 us
  transfers between devices with their start and end apart: 3, of which 3 were waited for; matrix products, arithmetic and copies ran while one was open for 1% of the time, Pallas kernels for 0%

commit v1 on v0

v1 whole, which is shorter than its diff:
```python
import math

import jax
import jax.numpy as jnp
from jax import lax
from jax.experimental import pallas as pl
from jax.experimental.pallas import tpu as pltpu
from jax.sharding import PartitionSpec as P

TAPS = 7
MODES = 16
LANES = 128
SUB = 8
PLANE = 8
HEAD = 8
GROUP = 8
HIGHEST = lax.Precision.HIGHEST
F32 = jnp.float32


def whole(memory_space=pltpu.VMEM):
    return pl.BlockSpec(memory_space=memory_space)


def spread(dst, base, src, rows):
    for j in range(SUB):
        dst[pl.ds(base * SUB + j, rows, stride=SUB), :] = src[:, j * LANES : (j + 1) * LANES]


def tile(ref, row):
    return ref[pl.ds(pl.multiple_of(row * SUB, SUB), SUB), :]


def tree_sum(parts):
    while len(parts) > 1:
        parts = [parts[k] + parts[k + 1] for k in range(0, len(parts), 2)]
    return parts[0]


def spread_modes(mode_s, rates, residues, length):
    spread(mode_s.at[0], 0, jnp.exp(rates[...] * (-1.0 / length)), MODES)
    spread(mode_s.at[1], 0, residues[...] * (1.0 / math.sqrt(length)), MODES)


def short_convs(xs, tap_s, first, base_out, query_out, at):
    done = []
    for g in range(3):
        window = [tile(xs.at[g], first - (TAPS - 1) + i) for i in range(GROUP + TAPS - 1)]
        weights = [tile(tap_s.at[g], j) for j in range(TAPS)]
        outs = []
        for i in range(GROUP):
            total = weights[0] * window[i + TAPS - 1]
            for j in range(1, TAPS):
                total = total + weights[j] * window[i + TAPS - 1 - j]
            outs.append(total)
        done.append(outs)
    for i in range(GROUP):
        query_out[at + i] = done[0][i]
        base_out[at + i] = (done[1][i] * done[2][i]).astype(jnp.bfloat16).astype(F32)


def scan(first, count, decay, weight, direct, state, base_out):
    state = list(state)
    for i in range(count):
        kv = base_out[first + i]
        state = [decay[n] * state[n] + kv for n in range(MODES)]
        base_out[first + i] = direct * kv + tree_sum(
            [weight[n] * state[n] for n in range(MODES)]
        )
    return tuple(state)


def rest_kernel(
    length, proj, taps, rates, residues, skip, state_out, base_out, query_out, xs, tap_s, mode_s
):
    rows = proj.shape[1]
    for g in range(3):
        spread(xs.at[g], 0, proj[g].astype(F32), rows)
        spread(tap_s.at[g], 0, taps[g], TAPS)
    spread_modes(mode_s, rates, residues, length)

    def conv_step(step, nothing):
        at = step * GROUP
        short_convs(xs, tap_s, at + HEAD, base_out, query_out, at)
        return nothing

    lax.fori_loop(0, (rows - HEAD) // GROUP, conv_step, 0)
    decay = [tile(mode_s.at[0], n) for n in range(MODES)]
    weight = [tile(mode_s.at[1], n) for n in range(MODES)]
    direct = skip[...]

    def scan_step(step, state):
        return scan(step * 4, 4, decay, weight, direct, state, base_out)

    zero = jnp.zeros((SUB, LANES), F32)
    state = lax.fori_loop(0, (rows - HEAD) // 4, scan_step, (zero,) * MODES)
    for n in range(MODES):
        state_out[n] = state[n]


def head_kernel(
    length,
    block,
    rim,
    proj,
    taps,
    rates,
    residues,
    skip,
    rest,
    state_out,
    enter_out,
    base_out,
    query_out,
    xs,
    tap_s,
    mode_s,
    fade_s,
):
    for g in range(3):
        spread(xs.at[g], 0, rim[g].astype(F32), HEAD)
        spread(xs.at[g], HEAD, proj[g].astype(F32)[:HEAD], HEAD)
        spread(tap_s.at[g], 0, taps[g], TAPS)
    spread_modes(mode_s, rates, residues, length)
    spread(fade_s, 0, jnp.exp(rates[...] * (-float(block - HEAD) / length)), MODES)
    short_convs(xs, tap_s, HEAD, base_out, query_out, 0)
    decay = [tile(mode_s.at[0], n) for n in range(MODES)]
    weight = [tile(mode_s.at[1], n) for n in range(MODES)]
    zero = jnp.zeros((SUB, LANES), F32)
    state = scan(0, HEAD, decay, weight, skip[...], (zero,) * MODES, base_out)
    for n in range(MODES):
        enter_out[n] = decay[n] * weight[n] * state[n]
        state_out[pl.ds(n, SUB, stride=MODES), :] = rest[n] + tile(fade_s, n) * state[n]


def own_columns(rates):
    at = lax.rem(lax.axis_index("ctx"), PLANE)
    return rates[:, pl.ds(pl.multiple_of(at * LANES, LANES), LANES)]


def total_kernel(block, length, planes, states, rates, total_out):
    step = jnp.exp(own_columns(rates) * (-float(block) / length))
    total = states[0]
    for p in range(1, PLANE):
        total = step * total + states[p]
    total = total.astype(total_out.dtype)
    for z in range(planes):
        total_out[z] = total


def carry_kernel(block, length, planes, totals, states, rates, carry_out):
    mine = lax.div(lax.axis_index("ctx"), PLANE)
    rate = own_columns(rates)
    carry = jnp.zeros((MODES, LANES), F32)
    for z in range(planes):
        gap = jnp.maximum(mine - 1 - z, 0).astype(F32) * (float(block * PLANE) / length)
        share = jnp.exp(-(rate * gap)) * totals[z].astype(F32)
        carry = carry + jnp.where(z < mine, share, 0.0)
    step = jnp.exp(rate * (-float(block) / length))
    for p in range(PLANE):
        carry_out[p] = carry
        carry = step * carry + states[p]


def gate_kernel(
    length,
    carry,
    rates,
    residues,
    enter,
    base_head,
    query_head,
    base,
    query,
    gated_out,
    squares_out,
    mode_s,
    tiles,
):
    rows = HEAD + base.shape[0]
    spread_modes(mode_s, rates, residues, length)
    decay = [tile(mode_s.at[0], n) for n in range(MODES)]
    state = [
        decay[n] * tile(mode_s.at[1], n) * carry[pl.ds(n, SUB, stride=MODES), :]
        for n in range(MODES)
    ]

    def four(first, base, query, at, state):
        for i in range(4):
            value = query[first + i] * (base[first + i] + tree_sum(list(state)))
            tiles[pl.ds(pl.multiple_of((at + i) * SUB, SUB), SUB), :] = value
            state = [decay[n] * state[n] for n in range(MODES)]
        return tuple(state)

    for at in range(0, HEAD, 4):
        state = four(at, base_head, query_head, at, state)
    state = tuple(state[n] + enter[n] for n in range(MODES))
    lax.fori_loop(
        0,
        (rows - HEAD) // 4,
        lambda step, held: four(step * 4, base, query, step * 4 + HEAD, held),
        state,
    )
    squares = jnp.zeros((rows, LANES), F32)
    for j in range(SUB):
        part = tiles[pl.ds(j, rows, stride=SUB), :]
        gated_out[:, j * LANES : (j + 1) * LANES] = part
        squares = squares + part * part
    ones = jnp.ones((SUB, LANES), F32)
    line = lax.dot_general(
        ones, squares, (((1,), (1,)), ((), ())), precision=HIGHEST, preferred_element_type=F32
    )
    squares_out[...] = line[: squares_out.shape[0]]


def norm_kernel(width, gated, squares, gain, out):
    count = squares.shape[0]
    ones = jnp.ones((count, LANES), F32)
    total = lax.dot_general(
        squares[...], ones, (((0,), (0,)), ((), ())), precision=HIGHEST, preferred_element_type=F32
    )
    scale = lax.rsqrt(total * (1.0 / width) + 1e-05)
    for j in range(SUB):
        cols = slice(j * LANES, (j + 1) * LANES)
        out[:, cols] = (gated[:, cols] * gain[:, cols] * scale).astype(out.dtype)


def on_chip(mebibytes):
    return pltpu.CompilerParams(vmem_limit_bytes=mebibytes << 20)


def array(*shape):
    return jax.ShapeDtypeStruct(shape, F32)


def shards(projected, short_taps, residues, rates, skip_gain, norm_gain):
    rows = projected.shape[0]
    channels = projected.shape[2]
    groups = lax.axis_size("ctx")
    parts = lax.axis_size("tp")
    planes = groups // PLANE
    length = rows * groups
    in_plane = [[z * PLANE + p for p in range(PLANE)] for z in range(planes)]
    along_z = [[z * PLANE + p for z in range(planes)] for p in range(PLANE)]

    proj = jnp.transpose(projected, (1, 0, 2))
    rate_t = rates.T
    residue_t = residues.T
    skip = skip_gain.reshape(SUB, LANES)
    rim = lax.ppermute(
        proj[:, rows - HEAD :], "ctx", [(i, i + 1) for i in range(groups - 1)]
    )
    tap_tiles = pltpu.VMEM((3, TAPS * SUB, LANES), F32)
    mode_tiles = pltpu.VMEM((2, MODES * SUB, LANES), F32)
    rest, base, query = pl.pallas_call(
        lambda *refs: rest_kernel(length, *refs),
        name="rest",
        out_shape=(
            array(MODES, SUB, LANES),
            array(rows - HEAD, SUB, LANES),
            array(rows - HEAD, SUB, LANES),
        ),
        in_specs=[whole()] * 5,
        out_specs=(whole(),) * 3,
        scratch_shapes=[pltpu.VMEM((3, rows * SUB, LANES), F32), tap_tiles, mode_tiles],
        compiler_params=on_chip(16),
        cost_estimate=pl.CostEstimate(
            flops=100 * rows * channels, bytes_accessed=4 << 20, transcendentals=0
        ),
    )(proj, short_taps, rate_t, residue_t, skip)
    states, enter, base_head, query_head = pl.pallas_call(
        lambda *refs: head_kernel(length, rows, *refs),
        name="head",
        out_shape=(
            array(SUB * MODES, LANES),
            array(MODES, SUB, LANES),
            array(HEAD, SUB, LANES),
            array(HEAD, SUB, LANES),
        ),
        grid=(1,),
        in_specs=[
            whole(),
            pl.BlockSpec((3, 16, channels), lambda i: (0, 0, 0)),
        ]
        + [whole()] * 5,
        out_specs=(whole(),) * 4,
        scratch_shapes=[
            pltpu.VMEM((3, 2 * HEAD * SUB, LANES), F32),
            tap_tiles,
            mode_tiles,
            pltpu.VMEM((MODES * SUB, LANES), F32),
        ],
        compiler_params=on_chip(8),
    )(rim, proj, short_taps, rate_t, residue_t, skip, rest)

    met = lax.all_to_all(
        states.reshape(SUB, MODES, LANES), "ctx", 0, 0, tiled=True, axis_index_groups=in_plane
    )
    totals = pl.pallas_call(
        lambda *refs: total_kernel(rows, length, planes, *refs),
        name="total",
        out_shape=jax.ShapeDtypeStruct((planes, MODES, LANES), jnp.bfloat16),
        in_specs=[whole()] * 2,
        out_specs=whole(),
        compiler_params=on_chip(4),
    )(met, rate_t)
    gathered = lax.all_to_all(totals, "ctx", 0, 0, tiled=True, axis_index_groups=along_z)
    carries = pl.pallas_call(
        lambda *refs: carry_kernel(rows, length, planes, *refs),
        name="carry",
        out_shape=array(PLANE, MODES, LANES),
        in_specs=[whole()] * 3,
        out_specs=whole(),
        compiler_params=on_chip(4),
    )(gathered, met, rate_t)
    carry = lax.all_to_all(carries, "ctx", 0, 0, tiled=True, axis_index_groups=in_plane)

    gated, squares = pl.pallas_call(
        lambda *refs: gate_kernel(length, *refs),
        name="gate",
        out_shape=(array(rows, channels), array(parts, rows)),
        in_specs=[whole()] * 8,
        out_specs=(whole(),) * 2,
        scratch_shapes=[mode_tiles, pltpu.VMEM((rows * SUB, LANES), F32)],
        compiler_params=on_chip(16),
    )(
        carry.reshape(SUB * MODES, LANES),
        rate_t,
        residue_t,
        enter,
        base_head,
        query_head,
        base,
        query,
    )
    squares = lax.all_to_all(squares, "tp", 0, 0, tiled=True)
    return pl.pallas_call(
        lambda *refs: norm_kernel(channels * parts, *refs),
        name="norm",
        out_shape=jax.ShapeDtypeStruct((rows, channels), jnp.bfloat16),
        in_specs=[whole()] * 3,
        out_specs=whole(),
        compiler_params=on_chip(4),
    )(gated, squares, norm_gain.reshape(1, channels))


def solution(mesh):
    return jax.shard_map(
        shards,
        mesh=mesh,
        in_specs=(
            P("ctx", None, "tp"),
            P(None, None, "tp"),
            P("tp", None),
            P("tp", None),
            P("tp"),
            P("tp"),
        ),
        out_specs=P("ctx", "tp"),
        check_vma=False,
    )
```

time: 78.3 us -> 66.6 us (0.85)
  blocking collectives: 18.5 us -> 52.9 us
  waiting for transfers between devices: 20.2 us -> 0.01 us
  starting transfers between devices: 24 us -> 4.63 us
  Pallas kernels: 9.39 us -> 4.79 us
  local copies, waits for them, and re-layouts: 5.54 us -> 3.71 us
    all_to_all x0 -> x2, blocking collectives: none -> 35 us  [the longest x1 24.2 us: shards(): lax.all_to_all(totals, 'ctx', 0, 0, tiled=True, axis_index_groups=along_z)]
    all_to_all x2 -> x0, starting transfers between devices: 19.5 us -> none  [the longest x1 16.1 us: shards(): lax.all_to_all(totals, 'ctx', 0, 0, tiled=True, axis_index_groups=along_z)]
    all_to_all x2 -> x0, waiting for transfers between devices: 15.8 us -> none  [the longest x1 11.6 us: shards(): lax.all_to_all(totals, 'ctx', 0, 0, tiled=True, axis_index_groups=along_z)]
    ppermute x1, waiting for transfers between devices: 4.33 us -> 0.01 us  [shards(): lax.ppermute(proj[:, rows - HEAD:], 'ctx', [(i, i + 1) for i in range(gro...]
    pallas_call x1, Pallas kernels: 1.57 us -> 0.07 us  [shards(): pl.pallas_call(lambda *refs: carry_kernel(rows, length, planes, *refs), n...]
    pallas_call x1, Pallas kernels: 1.49 us -> 0.03 us  [shards(): pl.pallas_call(lambda *refs: total_kernel(rows, length, planes, *refs), n...]
    unnamed x16 -> x14, local copies, waits for them, and re-layouts: 4.1 us -> 2.88 us
    pallas_call x1, Pallas kernels: 2.05 us -> 1.01 us  [shards(): pl.pallas_call(lambda *refs: norm_kernel(channels * parts, *refs), name='...]
  transfers between devices with their start and end apart: 3 -> 1, of which waited for: 3 -> 0; matrix products, arithmetic and copies ran while one was open for 1% -> 0% of each run, Pallas kernels for 0% -> 4%
where the time goes in v1:
time: 66.6 us; the launch traced here: 66.1 us
  blocking collectives  52.9 us (79%)
  Pallas kernels  4.79 us (7%)
  starting transfers between devices  4.63 us (7%)
  local copies, waits for them, and re-layouts  3.71 us (6%)
    all_to_all x1, blocking collectives, shards(): lax.all_to_all(totals, 'ctx', 0, 0, tiled=True, axis_index_groups=along_z)  24.2 us
    all_to_all x1, blocking collectives, shards(): lax.all_to_all(states.reshape(SUB, MODES, LANES), 'ctx', 0, 0, tiled=True...  10.9 us
    all_to_all x1, blocking collectives, shards(): lax.all_to_all(carries, 'ctx', 0, 0, tiled=True, axis_index_groups=in_plane)  9.57 us
    all_to_all x1, blocking collectives, shards(): squares = lax.all_to_all(squares, 'tp', 0, 0, tiled=True)  8.24 us
    ppermute x1, starting transfers between devices, shards(): lax.ppermute(proj[:, rows - HEAD:], 'ctx', [(i, i + 1) for i in range(gro...  4.63 us
    unnamed x14, local copies, waits for them, and re-layouts  2.88 us
    pallas_call x1, Pallas kernels, shards(): pl.pallas_call(lambda *refs: rest_kernel(length, *refs), name='rest', out...  2.51 us
  transfers between devices with their start and end apart: 1, of which 0 were waited for; matrix products, arithmetic and copies ran while one was open for 0% of the time, Pallas kernels for 4%

profile of v1, /device:TPU:1, one launch (start us, length us, event | category | flops | bytes accessed | tf_op | source)
XLA Modules:
  0.0 66.1 jit_solution(2801722348096175692)
XLA Ops:
  0.0 0.0 copy-start.1
  0.0 0.8 %slice.4 = bf16[3,8,1024]{2,1,0:T(8,128)(2,1)S(1)} slice(bf16[3,128,1024]{2,1,0:T(8,128)(2,1)} %bitcast.11), slice={[0:3], [120:128], [0:1024]} | slice | bytes 98304 | tf_op jit(solution)/shard_map/slice | solution.py:251
  0.8 0.0 copy-start.5
  0.8 4.6 %collective-permute-start = (bf16[3,8,1024]{2,1,0:T(8,128)(2,1)S(1)}, bf16[3,8,1024]{2,1,0:T(8,128)(2,1)S(1)}, u32[]{:S(2)}, u32[]{:S(2)}) collective-permute-start(bf16[3,8,1024]{2,1,0:T(8,128)(2,1)S(1)} %slice.4), channel_id=1, source_target_pairs={{0,4},{4,8},{8,12},{12,16},{16,20},{20,24},{24,28},{28,32},{32,36}... | collective-permute-start | bytes 147464 | tf_op jit(solution)/shard_map/ppermute | solution.py:250
  5.5 0.0 copy-done.1
  5.5 0.0 copy-done.5
  5.5 0.0 copy-start
  5.5 1.1 %copy-done = bf16[128,3,1024]{2,0,1:T(8,128)(2,1)S(1)} copy-done((bf16[128,3,1024]{2,0,1:T(8,128)(2,1)S(1)}, bf16[128,3,1024]{2,0,1:T(8,128)(2,1)}, u32[]{:S(2)}) %copy-start) | copy-done | bytes 786456
  6.6 0.0 copy-start.2
  6.6 0.8 %copy-done.2 = f32[1024,16]{0,1:T(8,128)S(1)} copy-done((f32[1024,16]{0,1:T(8,128)S(1)}, f32[1024,16]{0,1:T(8,128)}, u32[]{:S(2)}) %copy-start.2) | copy-done | bytes 65560
  7.5 0.9 %copy-done.4 = f32[3,7,1024]{2,1,0:T(8,128)S(1)} copy-done((f32[3,7,1024]{2,1,0:T(8,128)S(1)}, f32[3,7,1024]{2,1,0:T(8,128)}, u32[]{:S(2)}) %copy-start.4) | copy-done | bytes 86040
  8.4 2.5 %rest.1 = (f32[16,8,128]{2,1,0:T(8,128)S(1)}, f32[120,8,128]{2,1,0:T(8,128)S(1)}, f32[120,8,128]{2,1,0:T(8,128)S(1)}) custom-call(bf16[3,128,1024]{2,1,0:T(8,128)(2,1)S(1)} %bitcast.12, f32[3,7,1024]{2,1,0:T(8,128)S(1)} %copy-done.4, f32[16,1024]{1,0:T(8,128)S(1)} %bitcast.14, f32[16,1024]{1,0:T(8,128)S(1)} %bitcast.19, f32[8,128]{1,0:T(8,128)S(1)} %bitcast.24), custom_call_target="tpu_custom_call" | custom-call | flops 13107200 | bytes 4194304 | tf_op jit(solution)/shard_map/rest/pallas_call | solution.py:255
  10.9 0.0 collective-permute-done.refs_0_
  10.9 0.2 head.1
  11.1 10.9 %all_to_all.26.refs_0_.refs_1_ = f32[8,16,128]{2,1,0:T(8,128)S(1)} all-to-all(f32[8,16,128]{2,1,0:T(8,128)S(1)} %bitcast.23), channel_id=1, replica_groups={{0,4,8,12,16,20,24,28},{32,36,40,44,48,52,56,60},{64,68,72,76,80,84,88,..., dimensions={0} | all-to-all | bytes 131072 | tf_op jit(solution)/shard_map/all_to_all | solution.py:296
  22.0 24.2 %all_to_all.27.refs_0_ = bf16[16,16,128]{2,1,0:T(8,128)(2,1)S(1)} all-to-all(bf16[16,16,128]{2,1,0:T(8,128)(2,1)S(1)} %total.1), channel_id=1, replica_groups={{0,32,64,96,128,160,192,224,256,288,320,352,384,416,448,480},{4,36,68,1..., dimensions={0} | all-to-all | bytes 131072 | tf_op jit(solution)/shard_map/all_to_all | solution.py:307
  46.2 0.1 carry.1
  46.3 0.0 copy-start.3
  46.3 9.6 %all_to_all.28 = f32[8,16,128]{2,1,0:T(8,128)S(1)} all-to-all(f32[8,16,128]{2,1,0:T(8,128)S(1)} %carry.1), channel_id=1, replica_groups={{0,4,8,12,16,20,24,28},{32,36,40,44,48,52,56,60},{64,68,72,76,80,84,88,..., dimensions={0} | all-to-all | bytes 131072 | tf_op jit(solution)/shard_map/all_to_all | solution.py:316
  55.9 0.0 copy-done.3
  55.9 1.0 %gate.1 = (f32[128,1024]{1,0:T(8,128)S(1)}, f32[4,128]{1,0:T(4,128)S(1)}) custom-call(f32[128,128]{1,0:T(8,128)S(1)} %bitcast.22, f32[16,1024]{1,0:T(8,128)S(1)} %bitcast.18, f32[16,1024]{1,0:T(8,128)S(1)} %bitcast.21, f32[16,8,128]{2,1,0:T(8,128)S(1)} %get-tuple-element.16.refs_3_, f32[8,8,128]{2,1,0:T(8,128)S(1)} %get-tuple-element.17.refs_4_, ...), custom_call_target="tpu_custom_call" | custom-call | tf_op jit(solution)/shard_map/gate/pallas_call | solution.py:318
  56.8 8.2 %all_to_all.29 = f32[4,1,128]{2,1,0:T(1,128)S(1)} all-to-all(f32[4,1,128]{2,1,0:T(1,128)S(1)} %bitcast.28), channel_id=1, replica_groups=mesh['ctx'=128,'tp'=4] {'tp'}, dimensions={0} | all-to-all | bytes 4096 | tf_op jit(solution)/shard_map/all_to_all | solution.py:336
  65.1 0.0 copy-done.6
  65.1 1.0 %norm.1 = bf16[128,1024]{1,0:T(8,128)(2,1)} custom-call(f32[128,1024]{1,0:T(8,128)S(1)} %get-tuple-element.21.refs_0_, f32[4,128]{1,0:T(4,128)S(1)} %bitcast.26, f32[1,1024]{1,0:T(1,128)S(1)} %bitcast.27), custom_call_target="tpu_custom_call" | custom-call | tf_op jit(solution)/shard_map/norm/pallas_call | solution.py:337
  (3 shorter events, 0.0 us)
Async XLA Ops:
  0.0 5.5 %copy-start.1 = (f32[1024,16]{0,1:T(8,128)S(1)}, f32[1024,16]{0,1:T(8,128)}, u32[]{:S(2)}) copy-start(f32[1024,16]{0,1:T(8,128)} %param.9) | copy-start | bytes 196612
  0.8 4.7 %copy-start.5 = (f32[1024]{0:T(1024)S(1)}, f32[1024]{0:T(1024)}, u32[]{:S(2)}) copy-start(f32[1024]{0:T(1024)} %param.10) | copy-start | bytes 12292
  0.8 10.0 %collective-permute-start = (bf16[3,8,1024]{2,1,0:T(8,128)(2,1)S(1)}, bf16[3,8,1024]{2,1,0:T(8,128)(2,1)S(1)}, u32[]{:S(2)}, u32[]{:S(2)}) collective-permute-start(bf16[3,8,1024]{2,1,0:T(8,128)(2,1)S(1)} %slice.4), channel_id=1, source_target_pairs={{0,4},{4,8},{8,12},{12,16},{16,20},{20,24},{24,28},{28,32},{32,36}... | collective-permute-start | bytes 147464 | tf_op jit(solution)/shard_map/ppermute | solution.py:250
  5.5 1.1 %copy-start = (bf16[128,3,1024]{2,0,1:T(8,128)(2,1)S(1)}, bf16[128,3,1024]{2,0,1:T(8,128)(2,1)}, u32[]{:S(2)}) copy-start(bf16[128,3,1024]{2,0,1:T(8,128)(2,1)} %param.6) | copy-start | bytes 2359300
  6.6 0.8 %copy-start.2 = (f32[1024,16]{0,1:T(8,128)S(1)}, f32[1024,16]{0,1:T(8,128)}, u32[]{:S(2)}) copy-start(f32[1024,16]{0,1:T(8,128)} %param.8) | copy-start | bytes 196612
  7.5 0.9 %copy-start.4 = (f32[3,7,1024]{2,1,0:T(8,128)S(1)}, f32[3,7,1024]{2,1,0:T(8,128)}, u32[]{:S(2)}) copy-start(f32[3,7,1024]{2,1,0:T(8,128)} %refs_2_.1) | copy-start | bytes 258052
  46.3 9.6 %copy-start.3 = (f32[1024,16]{0,1:T(8,128)S(1)}, f32[1024,16]{0,1:T(8,128)}, u32[]{:S(2)}) copy-start(f32[1024,16]{0,1:T(8,128)} %param.8) | copy-start | bytes 196612
  56.8 8.2 %copy-start.6 = (f32[1024]{0:T(1024)S(1)}, f32[1024]{0:T(1024)}, u32[]{:S(2)}) copy-start(f32[1024]{0:T(1024)} %param.11) | copy-start | bytes 12292

commit v2 on v0

v2 whole, which is shorter than its diff:
```python
import math

import jax
import jax.numpy as jnp
from jax import lax
from jax.experimental import pallas as pl
from jax.experimental.pallas import tpu as pltpu
from jax.sharding import PartitionSpec as P

TAPS = 7
MODES = 16
LANES = 128
SUB = 8
OWNERS = 16
HALF = LANES // 2
HEAD = 8
GROUP = 8
FIRST, LAST, SENT = 8, 16, 32
BACK = 24
TAP_AT = 3 * HEAD
DECAY_AT = TAP_AT + 3 * TAPS
WEIGHT_AT = DECAY_AT + MODES
SKIP_AT = WEIGHT_AT + MODES
KEPT = SKIP_AT + 1
EARLY = 2
HIGHEST = lax.Precision.HIGHEST
F32 = jnp.float32
BF16 = jnp.bfloat16


def whole(memory_space=pltpu.VMEM):
    return pl.BlockSpec(memory_space=memory_space)


def spread(dst, base, src, rows):
    for j in range(SUB):
        dst[pl.ds(base * SUB + j, rows, stride=SUB), :] = src[:, j * LANES : (j + 1) * LANES]


def tile(ref, row):
    return ref[pl.ds(pl.multiple_of(row * SUB, SUB), SUB), :]


def tree_sum(parts):
    while len(parts) > 1:
        parts = [parts[k] + parts[k + 1] for k in range(0, len(parts), 2)]
    return parts[0]


def swap(x):
    return pltpu.roll(x, HALF, 1)


def paired(first, second):
    low = lax.broadcasted_iota(jnp.int32, first.shape, 1) < HALF
    return jnp.where(low, first, swap(second)), jnp.where(low, swap(first), second)


def short_conv(xs, kept, g, first):
    window = [tile(xs, first - (TAPS - 1) + i) for i in range(GROUP + TAPS - 1)]
    weights = [tile(kept, TAP_AT + g * TAPS + j) for j in range(TAPS)]
    outs = []
    for i in range(GROUP):
        total = weights[0] * window[i + TAPS - 1]
        for j in range(1, TAPS):
            total = total + weights[j] * window[i + TAPS - 1 - j]
        outs.append(total)
    return outs


def products(keys, values):
    return [(k * v).astype(BF16).astype(F32) for k, v in zip(keys, values)]


def constants(kept):
    decay = [tile(kept, DECAY_AT + n) for n in range(MODES)]
    weight = [tile(kept, WEIGHT_AT + n) for n in range(MODES)]
    return decay, weight, tile(kept, SKIP_AT)


def advance(first, count, decay, state, source):
    state = list(state)
    for i in range(count):
        kv = source[first + i]
        state = [decay[n] * state[n] + kv for n in range(MODES)]
    return tuple(state)


def scan(first, count, decay, weight, direct, state, source, dest):
    state = list(state)
    for i in range(count):
        kv = source[first + i]
        state = [decay[n] * state[n] + kv for n in range(MODES)]
        dest[first + i] = direct * kv + tree_sum([weight[n] * state[n] for n in range(MODES)])
    return tuple(state)


def nothing():
    return (jnp.zeros((SUB, LANES), F32),) * MODES


def is_early():
    return lax.axis_index("ctx") < EARLY * OWNERS


def local_kernel(
    length,
    proj_hbm,
    taps_hbm,
    rates_hbm,
    residues_hbm,
    skip_hbm,
    message_out,
    base_out,
    query_out,
    kept,
    proj,
    taps,
    rates,
    residues,
    xs,
    state_s,
    rows_s,
    arrived,
):
    pieces = [(proj_hbm.at[g], proj.at[g]) for g in (1, 2, 0)]
    pieces[2:2] = [
        (taps_hbm, taps),
        (rates_hbm, rates),
        (residues_hbm, residues),
        (skip_hbm, kept.at[pl.ds(SKIP_AT * SUB, SUB)]),
    ]
    copies = [
        pltpu.make_async_copy(src, dst, arrived.at[i]) for i, (src, dst) in enumerate(pieces)
    ]
    for copy in copies:
        copy.start()
    rows = proj.shape[1]
    for g, copy in ((1, copies[0]), (2, copies[1])):
        copy.wait()
        spread(xs.at[g], 0, proj[g].astype(F32), rows)
    for copy in copies[2:6]:
        copy.wait()
    for g in range(3):
        spread(kept, TAP_AT + g * TAPS, taps[g], TAPS)
    spread(kept, DECAY_AT, jnp.exp(rates[...] * (-1.0 / length)), MODES)
    spread(kept, WEIGHT_AT, residues[...] * (1.0 / math.sqrt(length)), MODES)
    copies[6].wait()
    spread(xs.at[0], 0, proj[0].astype(F32), rows)
    for g in range(3):
        kept[pl.ds(g * HEAD * SUB, HEAD * SUB), :] = xs[g, : HEAD * SUB, :]
    decay, weight, direct = constants(kept)

    def conv_step(step, early):
        at = step * GROUP
        kv = products(*(short_conv(xs.at[g], kept, g, at + HEAD) for g in (1, 2)))
        if early:
            query = short_conv(xs.at[0], kept, 0, at + HEAD)
        else:
            query = [tile(xs.at[0], at + HEAD + i) for i in range(GROUP)]
        for i in range(GROUP):
            base_out[at + i] = kv[i]
            query_out[at + i] = query[i]

    def finish(early):
        def conv(step, carried):
            conv_step(step, early)
            return carried

        def step_fn(step, state):
            if early:
                return scan(step * 4, 4, decay, weight, direct, state, base_out, base_out)
            return advance(step * 4, 4, decay, state, base_out)

        lax.fori_loop(0, (rows - HEAD) // GROUP, conv, 0)
        state = lax.fori_loop(0, (rows - HEAD) // 4, step_fn, nothing())
        for n in range(MODES):
            state_s[n] = state[n]

    early = is_early()
    pl.when(early)(lambda: finish(True))
    pl.when(jnp.logical_not(early))(lambda: finish(False))

    for n in range(SUB):
        for h, value in enumerate(paired(state_s[n], state_s[n + SUB])):
            rows_s[pl.ds(h * SENT + n, SUB, stride=2 * SENT), :] = value
    for j in range(SUB):
        cols = slice(j * LANES, (j + 1) * LANES)
        ends = [proj[g, rows - 16 :, cols].astype(F32)[16 - HEAD :] for g in range(3)]
        starts = [proj[g, :16, cols].astype(F32)[:HEAD] for g in range(3)]
        for at, (first, second) in (
            (FIRST, (starts[1], starts[2])),
            (LAST, (ends[1], ends[2])),
            (LAST + HEAD, (ends[0], ends[0])),
        ):
            for h, value in enumerate(paired(first, second)):
                rows_s[pl.ds((2 * j + h) * SENT + at, HEAD), :] = value
    for d in range(OWNERS):
        message_out[d] = rows_s[pl.ds(d * SENT, SENT), :].astype(BF16)


def owned(source, rows, row_s):
    spot = lax.rem(lax.axis_index("ctx"), OWNERS)
    lanes = pl.ds(pl.multiple_of(lax.div(spot, 2) * LANES, LANES), LANES)
    first, second = source(lanes)
    row_s[0, :rows] = first
    row_s[1, :rows] = second
    lower, upper = paired(row_s[0], row_s[1])
    return jnp.where(lax.rem(spot, 2) == 0, lower, upper)


def own_rates(rates, row_s):
    return owned(lambda lanes: (rates[:SUB, lanes], rates[SUB:, lanes]), SUB, row_s)


def own_taps(taps, row_s):
    return owned(lambda lanes: (taps[1, :, lanes], taps[2, :, lanes]), TAPS, row_s)


def edge_state(before, first, taps, fades):
    window = jnp.concatenate([before, first], 0)
    conv = taps[0:1] * first
    for j in range(1, TAPS):
        conv = conv + taps[j : j + 1] * window[HEAD - j : 2 * HEAD - j]
    product = (conv * swap(conv)).astype(BF16).astype(F32)
    total = fades[0] * product[0:1]
    for s in range(1, HEAD):
        total = total + fades[s] * product[s : s + 1]
    return total


def edge_fades(rate, block, length):
    return [jnp.exp(rate * (-float(block - 1 - s) / length)) for s in range(HEAD)]


def meet_kernel(block, length, teams, met, rates, taps, states_out, sent_out, row_s):
    rate = own_rates(rates, row_s)
    weights = own_taps(taps, row_s)
    fades = edge_fades(rate, block, length)
    step = jnp.exp(rate * (-float(block) / length))
    total = None
    before = None
    for d in range(OWNERS):
        rows = met[d].astype(F32)
        state = rows[:SUB]
        if d:
            state = state + edge_state(before, rows[FIRST : FIRST + HEAD], weights, fades)
        states_out[d] = state
        total = state if d == 0 else step * total + state
        before = rows[LAST : LAST + HEAD]
    ending = met[OWNERS - 1].astype(F32)[LAST:].astype(BF16)
    opening = met[0].astype(F32)[FIRST : FIRST + HEAD]
    beginning = jnp.concatenate([total, opening], 0).astype(BF16)
    for m in range(teams):
        sent_out[m, :16] = ending
        sent_out[m, 16:] = beginning


def carry_kernel(
    block, length, teams, gathered, states, met, rates, taps, kept, back_out, row_s, edge_s
):
    del kept
    mine = lax.div(lax.axis_index("ctx"), OWNERS)
    rate = own_rates(rates, row_s)
    weights = own_taps(taps, row_s)
    fades = edge_fades(rate, block, length)
    whole_team = float(block * OWNERS) / length
    to_end = jnp.exp(rate * (-float(block * (OWNERS - 1)) / length))
    carry = jnp.zeros((SUB, LANES), F32)
    before = jnp.zeros((HEAD, LANES), F32)
    edge_s[0, :HEAD] = before
    edge_s[0, HEAD : 2 * HEAD] = before
    for m in range(teams):
        rows = gathered[m].astype(F32)
        edge = edge_state(before, rows[24:], weights, fades)
        edge_s[m, 2 * HEAD :] = edge
        gap = jnp.maximum(mine - 1 - m, 0).astype(F32) * whole_team
        share = jnp.exp(-(rate * gap)) * (rows[16:24] + to_end * edge)
        carry = carry + jnp.where(m < mine, share, 0.0)
        before = rows[:HEAD]
        if m + 1 < teams:
            edge_s[m + 1, : 2 * HEAD] = rows[: 2 * HEAD]
    step = jnp.exp(rate * (-float(block) / length))
    here = edge_s[mine]
    for d in range(OWNERS):
        if d == 0:
            ahead = here[: 2 * HEAD]
        else:
            ahead = met[d - 1].astype(F32)[LAST:]
        back_out[d] = jnp.concatenate([carry, ahead], 0).astype(BF16)
        state = states[d]
        if d == 0:
            state = state + here[2 * HEAD :]
        carry = step * carry + state


def gate_kernel(
    back,
    kept,
    base,
    query,
    gated_out,
    squares_out,
    xs,
    base_head,
    query_head,
    rows_s,
    tiles,
    raw_s,
    base_s,
    query_s,
):
    rest = base.shape[0]
    rows = HEAD + rest
    for g in range(3):
        xs[g, HEAD * SUB :] = kept[pl.ds(g * HEAD * SUB, HEAD * SUB), :]
    for d in range(OWNERS):
        rows_s[pl.ds(d * BACK, BACK), :] = back[d].astype(F32)

    def received(row):
        return paired(
            rows_s[pl.ds(row, SUB, stride=2 * BACK), :],
            rows_s[pl.ds(BACK + row, SUB, stride=2 * BACK), :],
        )

    for r in range(HEAD):
        key, value = received(SUB + r)
        xs[1, r * SUB : (r + 1) * SUB] = key
        xs[2, r * SUB : (r + 1) * SUB] = value
        xs[0, r * SUB : (r + 1) * SUB] = received(SUB + HEAD + r)[0]
    kv = products(*(short_conv(xs.at[g], kept, g, HEAD) for g in (1, 2)))
    for i, value in enumerate(short_conv(xs.at[0], kept, 0, HEAD)):
        query_head[i] = value
        base_head[i] = kv[i]
    decay, weight, direct = constants(kept)
    entered = scan(0, HEAD, decay, weight, direct, nothing(), base_head, base_head)
    state = [None] * MODES
    for n in range(SUB):
        for value, m in zip(received(n), (n, n + SUB)):
            state[m] = decay[m] * weight[m] * value

    def four(first, base, query, at, state):
        for i in range(4):
            value = query[first + i] * (base[first + i] + tree_sum(list(state)))
            tiles[pl.ds(pl.multiple_of((at + i) * SUB, SUB), SUB), :] = value
            state = [decay[n] * state[n] for n in range(MODES)]
        return tuple(state)

    for at in range(0, HEAD, 4):
        state = four(at, base_head, query_head, at, state)
    state = tuple(state[n] + decay[n] * weight[n] * entered[n] for n in range(MODES))

    def apply(base, query):
        lax.fori_loop(
            0,
            rest // 4,
            lambda step, held: four(step * 4, base, query, step * 4 + HEAD, held),
            state,
        )

    def own_output():
        raw_s[: HEAD * SUB] = xs[0, HEAD * SUB :]

        def lay(step, carried):
            for i in range(GROUP):
                row = step * GROUP + i
                raw_s[pl.ds(pl.multiple_of((row + HEAD) * SUB, SUB), SUB), :] = query[row]
            return carried

        def conv(step, carried):
            at = step * GROUP
            for i, value in enumerate(short_conv(raw_s, kept, 0, at + HEAD)):
                query_s[at + i] = value
            return carried

        lax.fori_loop(0, rest // GROUP, lay, 0)
        lax.fori_loop(0, rest // GROUP, conv, 0)
        lax.fori_loop(
            0,
            rest // 4,
            lambda step, held: scan(step * 4, 4, decay, weight, direct, held, base, base_s),
            nothing(),
        )
        apply(base_s, query_s)

    early = is_early()
    pl.when(early)(lambda: apply(base, query))
    pl.when(jnp.logical_not(early))(own_output)
    squares = jnp.zeros((rows, LANES), F32)
    for j in range(SUB):
        part = tiles[pl.ds(j, rows, stride=SUB), :]
        gated_out[:, j * LANES : (j + 1) * LANES] = part
        squares = squares + part * part
    ones = jnp.ones((SUB, LANES), F32)
    line = lax.dot_general(
        ones, squares, (((1,), (1,)), ((), ())), precision=HIGHEST, preferred_element_type=F32
    )
    squares_out[...] = line[: squares_out.shape[0]]


def norm_kernel(width, gated, squares, gain, out):
    count = squares.shape[0]
    ones = jnp.ones((count, LANES), F32)
    total = lax.dot_general(
        squares[...], ones, (((0,), (0,)), ((), ())), precision=HIGHEST, preferred_element_type=F32
    )
    scale = lax.rsqrt(total * (1.0 / width) + 1e-05)
    for j in range(SUB):
        cols = slice(j * LANES, (j + 1) * LANES)
        out[:, cols] = (gated[:, cols] * gain[:, cols] * scale).astype(out.dtype)


def on_chip(mebibytes):
    return pltpu.CompilerParams(vmem_limit_bytes=mebibytes << 20)


def array(*shape):
    return jax.ShapeDtypeStruct(shape, F32)


def shards(projected, short_taps, residues, rates, skip_gain, norm_gain):
    rows = projected.shape[0]
    channels = projected.shape[2]
    groups = lax.axis_size("ctx")
    parts = lax.axis_size("tp")
    teams = groups // OWNERS
    length = rows * groups
    in_team = [[m * OWNERS + d for d in range(OWNERS)] for m in range(teams)]
    across = [[m * OWNERS + d for m in range(teams)] for d in range(OWNERS)]

    proj = jnp.transpose(projected, (1, 0, 2))
    rate_t = rates.T
    residue_t = residues.T
    skip = skip_gain.reshape(SUB, LANES)
    block_tiles = pltpu.VMEM((rows - HEAD, SUB, LANES), F32)
    head_tiles = pltpu.VMEM((HEAD, SUB, LANES), F32)
    row_pair = pltpu.VMEM((2, SUB, LANES), F32)
    inputs = (proj, short_taps, rate_t, residue_t, skip)
    message, base, query, kept = pl.pallas_call(
        lambda *refs: local_kernel(length, *refs),
        name="local",
        out_shape=(
            jax.ShapeDtypeStruct((OWNERS, SENT, LANES), BF16),
            array(rows - HEAD, SUB, LANES),
            array(rows - HEAD, SUB, LANES),
            array(KEPT * SUB, LANES),
        ),
        in_specs=[whole(pltpu.HBM)] * 5,
        out_specs=(whole(),) * 4,
        scratch_shapes=[pltpu.VMEM(x.shape, x.dtype) for x in inputs[:4]]
        + [
            pltpu.VMEM((3, rows * SUB, LANES), F32),
            pltpu.VMEM((MODES, SUB, LANES), F32),
            pltpu.VMEM((OWNERS * SENT, LANES), F32),
            pltpu.SemaphoreType.DMA((7,)),
        ],
        compiler_params=on_chip(54),
    )(*inputs)

    met = lax.all_to_all(message, "ctx", 0, 0, tiled=True, axis_index_groups=in_team)
    states, sent = pl.pallas_call(
        lambda *refs: meet_kernel(rows, length, teams, *refs),
        name="meet",
        out_shape=(
            array(OWNERS, SUB, LANES),
            jax.ShapeDtypeStruct((teams, 4 * HEAD, LANES), BF16),
        ),
        in_specs=[whole()] * 3,
        out_specs=(whole(),) * 2,
        scratch_shapes=[row_pair],
        compiler_params=on_chip(4),
    )(met, rate_t, short_taps)
    gathered = lax.all_to_all(sent, "ctx", 0, 0, tiled=True, axis_index_groups=across)
    back = pl.pallas_call(
        lambda *refs: carry_kernel(rows, length, teams, *refs),
        name="carry",
        out_shape=jax.ShapeDtypeStruct((OWNERS, BACK, LANES), BF16),
        in_specs=[whole()] * 6,
        out_specs=whole(),
        scratch_shapes=[row_pair, pltpu.VMEM((teams, 3 * HEAD, LANES), F32)],
        compiler_params=on_chip(4),
    )(gathered, states, met, rate_t, short_taps, kept)
    back = lax.all_to_all(back, "ctx", 0, 0, tiled=True, axis_index_groups=in_team)

    gated, squares = pl.pallas_call(
        gate_kernel,
        name="gate",
        out_shape=(array(rows, channels), array(parts, rows)),
        in_specs=[whole()] * 4,
        out_specs=(whole(),) * 2,
        scratch_shapes=[
            pltpu.VMEM((3, 2 * HEAD * SUB, LANES), F32),
            head_tiles,
            head_tiles,
            pltpu.VMEM((OWNERS * BACK, LANES), F32),
            pltpu.VMEM((rows * SUB, LANES), F32),
            pltpu.VMEM((rows * SUB, LANES), F32),
            block_tiles,
            block_tiles,
        ],
        compiler_params=on_chip(16),
    )(back, kept, base, query)
    squares = lax.all_to_all(squares, "tp", 0, 0, tiled=True)
    return pl.pallas_call(
        lambda *refs: norm_kernel(channels * parts, *refs),
        name="norm",
        out_shape=jax.ShapeDtypeStruct((rows, channels), BF16),
        in_specs=[whole()] * 3,
        out_specs=whole(),
        compiler_params=on_chip(4),
    )(gated, squares, norm_gain.reshape(1, channels))


def solution(mesh):
    return jax.shard_map(
        shards,
        mesh=mesh,
        in_specs=(
            P("ctx", None, "tp"),
            P(None, None, "tp"),
            P("tp", None),
            P("tp", None),
            P("tp"),
            P("tp"),
        ),
        out_specs=P("ctx", "tp"),
        check_vma=False,
    )
```

time: 78.3 us -> 65.5 us (0.84)
  blocking collectives: 18.5 us -> 57.9 us
  starting transfers between devices: 24 us -> 0 us
  waiting for transfers between devices: 20.2 us -> 0 us
  local copies, waits for them, and re-layouts: 5.54 us -> 0.02 us
  Pallas kernels: 9.39 us -> 7.26 us
    all_to_all x1 -> x3, blocking collectives: 10.3 us -> 49.6 us  [the longest x1 21.9 us: shards(): lax.all_to_all(sent, 'ctx', 0, 0, tiled=True, axis_index_groups=across)]
    all_to_all x2 -> x0, starting transfers between devices: 19.5 us -> none  [the longest x1 16.1 us: shards(): lax.all_to_all(totals, 'ctx', 0, 0, tiled=True, axis_index_groups=along_z)]
    all_to_all x2 -> x0, waiting for transfers between devices: 15.8 us -> none  [the longest x1 11.6 us: shards(): lax.all_to_all(totals, 'ctx', 0, 0, tiled=True, axis_index_groups=along_z)]
    ppermute x1 -> x0, starting transfers between devices: 4.5 us -> none  [shards(): lax.ppermute(proj[:, rows - RIM:], 'ctx', [(i, i + 1) for i in range(grou...]
    ppermute x1 -> x0, waiting for transfers between devices: 4.33 us -> none  [shards(): lax.ppermute(proj[:, rows - RIM:], 'ctx', [(i, i + 1) for i in range(grou...]
    unnamed x16 -> x12, local copies, waits for them, and re-layouts: 4.1 us -> 0.02 us
    pallas_call x3, Pallas kernels: 4.02 us -> 1.63 us  [the longest x1 1.13 us: shards(): pl.pallas_call(gate_kernel, name='gate', out_shape=(array(rows, channels)...]
    pallas_call x1, Pallas kernels: 3.31 us -> 4.62 us  [shards(): pl.pallas_call(lambda *refs: local_kernel(length, *refs), name='local', o...]
  transfers between devices with their start and end apart: 3 -> 0, of which waited for: 3 -> 0; matrix products, arithmetic and copies ran while one was open for 1% -> 0% of each run, Pallas kernels for 0% -> 0%
where the time goes in v2:
time: 65.5 us; the launch traced here: 65.2 us
  blocking collectives  57.9 us (88%)
  Pallas kernels  7.26 us (11%)
    all_to_all x1, blocking collectives, shards(): lax.all_to_all(sent, 'ctx', 0, 0, tiled=True, axis_index_groups=across)  21.9 us
    all_to_all x1, blocking collectives, shards(): lax.all_to_all(message, 'ctx', 0, 0, tiled=True, axis_index_groups=in_team)  16.5 us
    all_to_all x1, blocking collectives, shards(): lax.all_to_all(back, 'ctx', 0, 0, tiled=True, axis_index_groups=in_team)  11.2 us
    all_to_all x1, blocking collectives, shards(): squares = lax.all_to_all(squares, 'tp', 0, 0, tiled=True)  8.24 us
    pallas_call x1, Pallas kernels, shards(): pl.pallas_call(lambda *refs: local_kernel(length, *refs), name='local', o...  4.62 us

profile of v2, /device:TPU:1, one launch (start us, length us, event | category | flops | bytes accessed | tf_op | source)
XLA Modules:
  0.0 65.2 jit_solution(9781238341777421593)
XLA Ops:
  0.0 0.0 copy-start.1
  0.0 0.0 copy-start.2
  0.0 4.6 %local.1 = (bf16[16,32,128]{2,1,0:T(8,128)(2,1)}, f32[120,8,128]{2,1,0:T(8,128)}, f32[120,8,128]{2,1,0:T(8,128)}, f32[624,128]{1,0:T(8,128)}) custom-call(bf16[3,128,1024]{2,1,0:T(8,128)(2,1)} %bitcast.15, f32[3,7,1024]{2,1,0:T(8,128)} %refs_4_.1, f32[16,1024]{1,0:T(8,128)} %bitcast.9, f32[16,1024]{1,0:T(8,128)} %bitcast.16, f32[8,128]{1,0:T(8,128)} %bitcast.17), custom_call_target="tpu_custom_call" | custom-call | tf_op jit(solution)/shard_map/local/pallas_call | solution.py:439
  4.6 0.0 copy-start
  4.6 16.5 %all_to_all.26.refs_0_.refs_2_ = bf16[16,32,128]{2,1,0:T(8,128)(2,1)S(1)} all-to-all(bf16[16,32,128]{2,1,0:T(8,128)(2,1)} %get-tuple-element.13), channel_id=1, replica_groups={{0,4,8,12,16,20,24,28,32,36,40,44,48,52,56,60},{64,68,72,76,80,84,88,92..., dimensions={0} | all-to-all | bytes 262144 | tf_op jit(solution)/shard_map/all_to_all | solution.py:460
  21.2 0.0 copy-done.1
  21.2 0.0 copy-done.2
  21.2 0.3 meet.1
  21.4 21.9 %all_to_all.27.refs_0_ = bf16[8,32,128]{2,1,0:T(8,128)(2,1)S(1)} all-to-all(bf16[8,32,128]{2,1,0:T(8,128)(2,1)S(1)} %get-tuple-element.14), channel_id=1, replica_groups={{0,64,128,192,256,320,384,448},{4,68,132,196,260,324,388,452},{8,72,136..., dimensions={0} | all-to-all | bytes 131072 | tf_op jit(solution)/shard_map/all_to_all | solution.py:473
  43.4 0.0 copy-done
  43.4 0.0 copy-start.3
  43.4 0.0 copy-start.4
  43.4 0.3 carry.1
  43.6 11.2 %all_to_all.28.back = bf16[16,24,128]{2,1,0:T(8,128)(2,1)S(1)} all-to-all(bf16[16,24,128]{2,1,0:T(8,128)(2,1)S(1)} %carry.1), channel_id=1, replica_groups={{0,4,8,12,16,20,24,28,32,36,40,44,48,52,56,60},{64,68,72,76,80,84,88,92..., dimensions={0} | all-to-all | bytes 196608 | tf_op jit(solution)/shard_map/all_to_all | solution.py:483
  54.8 0.0 copy-done.3
  54.8 0.0 copy-done.4
  54.8 1.1 %gate.1 = (f32[128,1024]{1,0:T(8,128)S(1)}, f32[4,128]{1,0:T(4,128)S(1)}) custom-call(bf16[16,24,128]{2,1,0:T(8,128)(2,1)S(1)} %all_to_all.28.back, f32[624,128]{1,0:T(8,128)S(1)} %copy-done, f32[120,8,128]{2,1,0:T(8,128)S(1)} %copy-done.3, f32[120,8,128]{2,1,0:T(8,128)S(1)} %copy-done.4), custom_call_target="tpu_custom_call" | custom-call | tf_op jit(solution)/shard_map/gate/pallas_call | solution.py:485
  55.9 0.0 copy-start.5
  55.9 8.2 %all_to_all.29 = f32[4,1,128]{2,1,0:T(1,128)S(1)} all-to-all(f32[4,1,128]{2,1,0:T(1,128)S(1)} %bitcast.14), channel_id=1, replica_groups=mesh['ctx'=128,'tp'=4] {'tp'}, dimensions={0} | all-to-all | bytes 4096 | tf_op jit(solution)/shard_map/all_to_all | solution.py:503
  64.2 0.0 copy-done.5
  64.2 1.0 %norm.1 = bf16[128,1024]{1,0:T(8,128)(2,1)} custom-call(f32[128,1024]{1,0:T(8,128)S(1)} %get-tuple-element.19.refs_0_, f32[4,128]{1,0:T(4,128)S(1)} %bitcast.12, f32[1,1024]{1,0:T(1,128)S(1)} %bitcast.13), custom_call_target="tpu_custom_call" | custom-call | tf_op jit(solution)/shard_map/norm/pallas_call | solution.py:504
Async XLA Ops:
  0.0 21.2 %copy-start.1 = (f32[3,7,1024]{2,1,0:T(8,128)S(1)}, f32[3,7,1024]{2,1,0:T(8,128)}, u32[]{:S(2)}) copy-start(f32[3,7,1024]{2,1,0:T(8,128)} %refs_4_.1) | copy-start | bytes 258052
  0.0 21.2 %copy-start.2 = (f32[1024,16]{0,1:T(8,128)S(1)}, f32[1024,16]{0,1:T(8,128)}, u32[]{:S(2)}) copy-start(f32[1024,16]{0,1:T(8,128)} %param.9) | copy-start | bytes 196612
  4.6 38.8 %copy-start = (f32[624,128]{1,0:T(8,128)S(1)}, f32[624,128]{1,0:T(8,128)}, u32[]{:S(2)}) copy-start(f32[624,128]{1,0:T(8,128)} %get-tuple-element.16.refs_5_.kept) | copy-start | bytes 958468
  43.4 11.4 %copy-start.3 = (f32[120,8,128]{2,1,0:T(8,128)S(1)}, f32[120,8,128]{2,1,0:T(8,128)}, u32[]{:S(2)}) copy-start(f32[120,8,128]{2,1,0:T(8,128)} %get-tuple-element.17.base) | copy-start | bytes 1474564
  43.4 11.4 %copy-start.4 = (f32[120,8,128]{2,1,0:T(8,128)S(1)}, f32[120,8,128]{2,1,0:T(8,128)}, u32[]{:S(2)}) copy-start(f32[120,8,128]{2,1,0:T(8,128)} %get-tuple-element.18.query) | copy-start | bytes 1474564
  55.9 8.2 %copy-start.5 = (f32[1024]{0:T(1024)S(1)}, f32[1024]{0:T(1024)}, u32[]{:S(2)}) copy-start(f32[1024]{0:T(1024)} %param.11) | copy-start | bytes 12292

commit v3 on v2

--- a/solution.py
+++ b/solution.py
@@ -114,6 +114,7 @@
     base_out,
     query_out,
     kept,
+    raw_out,
     proj,
     taps,
     rates,
@@ -123,7 +124,12 @@
     rows_s,
     arrived,
 ):
-    pieces = [(proj_hbm.at[g], proj.at[g]) for g in (1, 2, 0)]
+    pieces = [
+        (proj_hbm.at[1], proj.at[0]),
+        (proj_hbm.at[2], proj.at[1]),
+        (proj_hbm.at[0], raw_out),
+    ]
+    projections = (raw_out, proj.at[0], proj.at[1])
     pieces[2:2] = [
         (taps_hbm, taps),
         (rates_hbm, rates),
@@ -135,10 +141,10 @@
     ]
     for copy in copies:
         copy.start()
-    rows = proj.shape[1]
+    rows = raw_out.shape[0]
     for g, copy in ((1, copies[0]), (2, copies[1])):
         copy.wait()
-        spread(xs.at[g], 0, proj[g].astype(F32), rows)
+        spread(xs.at[g], 0, projections[g][...].astype(F32), rows)
     for copy in copies[2:6]:
         copy.wait()
     for g in range(3):
@@ -146,7 +152,9 @@
     spread(kept, DECAY_AT, jnp.exp(rates[...] * (-1.0 / length)), MODES)
     spread(kept, WEIGHT_AT, residues[...] * (1.0 / math.sqrt(length)), MODES)
     copies[6].wait()
-    spread(xs.at[0], 0, proj[0].astype(F32), rows)
+    early = is_early()
+    spread(xs.at[0], 0, raw_out[:16].astype(F32), 16)
+    pl.when(early)(lambda: spread(xs.at[0], 0, raw_out[...].astype(F32), rows))
     for g in range(3):
         kept[pl.ds(g * HEAD * SUB, HEAD * SUB), :] = xs[g, : HEAD * SUB, :]
     decay, weight, direct = constants(kept)
@@ -154,13 +162,11 @@
     def conv_step(step, early):
         at = step * GROUP
         kv = products(*(short_conv(xs.at[g], kept, g, at + HEAD) for g in (1, 2)))
-        if early:
-            query = short_conv(xs.at[0], kept, 0, at + HEAD)
-        else:
-            query = [tile(xs.at[0], at + HEAD + i) for i in range(GROUP)]
         for i in range(GROUP):
             base_out[at + i] = kv[i]
-            query_out[at + i] = query[i]
+        if early:
+            for i, value in enumerate(short_conv(xs.at[0], kept, 0, at + HEAD)):
+                query_out[at + i] = value
 
     def finish(early):
         def conv(step, carried):
@@ -177,7 +183,6 @@
         for n in range(MODES):
             state_s[n] = state[n]
 
-    early = is_early()
     pl.when(early)(lambda: finish(True))
     pl.when(jnp.logical_not(early))(lambda: finish(False))
 
@@ -186,8 +191,8 @@
             rows_s[pl.ds(h * SENT + n, SUB, stride=2 * SENT), :] = value
     for j in range(SUB):
         cols = slice(j * LANES, (j + 1) * LANES)
-        ends = [proj[g, rows - 16 :, cols].astype(F32)[16 - HEAD :] for g in range(3)]
-        starts = [proj[g, :16, cols].astype(F32)[:HEAD] for g in range(3)]
+        ends = [x[rows - 16 :, cols].astype(F32)[16 - HEAD :] for x in projections]
+        starts = [x[:16, cols].astype(F32)[:HEAD] for x in projections]
         for at, (first, second) in (
             (FIRST, (starts[1], starts[2])),
             (LAST, (ends[1], ends[2])),
@@ -256,10 +261,7 @@
         sent_out[m, 16:] = beginning
 
 
-def carry_kernel(
-    block, length, teams, gathered, states, met, rates, taps, kept, back_out, row_s, edge_s
-):
-    del kept
+def carry_kernel(block, length, teams, gathered, states, met, rates, taps, back_out, row_s, edge_s):
     mine = lax.div(lax.axis_index("ctx"), OWNERS)
     rate = own_rates(rates, row_s)
     weights = own_taps(taps, row_s)
@@ -299,6 +301,7 @@
     kept,
     base,
     query,
+    raw,
     gated_out,
     squares_out,
     xs,
@@ -359,13 +362,7 @@
         )
 
     def own_output():
-        raw_s[: HEAD * SUB] = xs[0, HEAD * SUB :]
-
-        def lay(step, carried):
-            for i in range(GROUP):
-                row = step * GROUP + i
-                raw_s[pl.ds(pl.multiple_of((row + HEAD) * SUB, SUB), SUB), :] = query[row]
-            return carried
+        spread(raw_s, 0, raw[...].astype(F32), rows)
 
         def conv(step, carried):
             at = step * GROUP
@@ -373,7 +370,6 @@
                 query_s[at + i] = value
             return carried
 
-        lax.fori_loop(0, rest // GROUP, lay, 0)
         lax.fori_loop(0, rest // GROUP, conv, 0)
         lax.fori_loop(
             0,
@@ -436,7 +432,7 @@
     head_tiles = pltpu.VMEM((HEAD, SUB, LANES), F32)
     row_pair = pltpu.VMEM((2, SUB, LANES), F32)
     inputs = (proj, short_taps, rate_t, residue_t, skip)
-    message, base, query, kept = pl.pallas_call(
+    message, base, query, kept, raw = pl.pallas_call(
         lambda *refs: local_kernel(length, *refs),
         name="local",
         out_shape=(
@@ -444,18 +440,20 @@
             array(rows - HEAD, SUB, LANES),
             array(rows - HEAD, SUB, LANES),
             array(KEPT * SUB, LANES),
+            jax.ShapeDtypeStruct((rows, channels), BF16),
         ),
         in_specs=[whole(pltpu.HBM)] * 5,
-        out_specs=(whole(),) * 4,
-        scratch_shapes=[pltpu.VMEM(x.shape, x.dtype) for x in inputs[:4]]
+        out_specs=(whole(),) * 5,
+        scratch_shapes=[pltpu.VMEM((2, rows, channels), BF16)]
+        + [pltpu.VMEM(x.shape, x.dtype) for x in inputs[1:4]]
         + [
             pltpu.VMEM((3, rows * SUB, LANES), F32),
             pltpu.VMEM((MODES, SUB, LANES), F32),
             pltpu.VMEM((OWNERS * SENT, LANES), F32),
             pltpu.SemaphoreType.DMA((7,)),
         ],
-        compiler_params=on_chip(54),
-    )(*inputs)
+        compiler_params=on_chip(32),
+    )(*(pltpu.with_memory_space_constraint(x, pltpu.HBM) for x in inputs))
 
     met = lax.all_to_all(message, "ctx", 0, 0, tiled=True, axis_index_groups=in_team)
     states, sent = pl.pallas_call(
@@ -475,18 +473,18 @@
         lambda *refs: carry_kernel(rows, length, teams, *refs),
         name="carry",
         out_shape=jax.ShapeDtypeStruct((OWNERS, BACK, LANES), BF16),
-        in_specs=[whole()] * 6,
+        in_specs=[whole()] * 5,
         out_specs=whole(),
         scratch_shapes=[row_pair, pltpu.VMEM((teams, 3 * HEAD, LANES), F32)],
         compiler_params=on_chip(4),
-    )(gathered, states, met, rate_t, short_taps, kept)
+    )(gathered, states, met, rate_t, short_taps)
     back = lax.all_to_all(back, "ctx", 0, 0, tiled=True, axis_index_groups=in_team)
 
     gated, squares = pl.pallas_call(
         gate_kernel,
         name="gate",
         out_shape=(array(rows, channels), array(parts, rows)),
-        in_specs=[whole()] * 4,
+        in_specs=[whole()] * 5,
         out_specs=(whole(),) * 2,
         scratch_shapes=[
             pltpu.VMEM((3, 2 * HEAD * SUB, LANES), F32),
@@ -499,7 +497,7 @@
             block_tiles,
         ],
         compiler_params=on_chip(16),
-    )(back, kept, base, query)
+    )(back, kept, base, query, raw)
     squares = lax.all_to_all(squares, "tp", 0, 0, tiled=True)
     return pl.pallas_call(
         lambda *refs: norm_kernel(channels * parts, *refs),

time: 65.5 us -> 64.1 us (0.979)
  Pallas kernels: 7.26 us -> 6.23 us
    pallas_call x1, Pallas kernels: 4.62 us -> 3.6 us  [shards(): pl.pallas_call(lambda *refs: local_kernel(length, *refs), name='local', o...]
    all_to_all x1, blocking collectives: 16.5 us -> 15.6 us  [shards(): lax.all_to_all(message, 'ctx', 0, 0, tiled=True, axis_index_groups=in_team)]
where the time goes in v3:
time: 64.1 us; the launch traced here: 63.8 us
  blocking collectives  57.5 us (90%)
  Pallas kernels  6.23 us (10%)
    all_to_all x1, blocking collectives, shards(): lax.all_to_all(sent, 'ctx', 0, 0, tiled=True, axis_index_groups=across)  22.6 us
    all_to_all x1, blocking collectives, shards(): lax.all_to_all(message, 'ctx', 0, 0, tiled=True, axis_index_groups=in_team)  15.6 us
    all_to_all x1, blocking collectives, shards(): lax.all_to_all(back, 'ctx', 0, 0, tiled=True, axis_index_groups=in_team)  11 us
    all_to_all x1, blocking collectives, shards(): squares = lax.all_to_all(squares, 'tp', 0, 0, tiled=True)  8.24 us
    pallas_call x1, Pallas kernels, shards(): pl.pallas_call(lambda *refs: local_kernel(length, *refs), name='local', o...  3.6 us

profile of v3, /device:TPU:1, one launch (start us, length us, event | category | flops | bytes accessed | tf_op | source)
XLA Modules:
  0.0 63.8 jit_solution(8884398494783475406)
XLA Ops:
  0.0 3.6 %local.1 = (bf16[16,32,128]{2,1,0:T(8,128)(2,1)S(1)}, f32[120,8,128]{2,1,0:T(8,128)S(1)}, f32[120,8,128]{2,1,0:T(8,128)S(1)}, f32[624,128]{1,0:T(8,128)S(1)}, bf16[128,1024]{1,0:T(8,128)(2,1)S(1)}) custom-call(bf16[3,128,1024]{2,1,0:T(8,128)(2,1)} %bitcast.15, f32[3,7,1024]{2,1,0:T(8,128)} %refs_4_.1, f32[16,1024]{1,0:T(8,128)} %bitcast.9, ...), custom_call_target="tpu_custom_call" | custom-call | tf_op jit(solution)/shard_map/local/pallas_call | solution.py:435
  3.6 0.0 copy-start
  3.6 0.0 copy-start.1
  3.6 15.6 %all_to_all.26.refs_0_.refs_2_ = bf16[16,32,128]{2,1,0:T(8,128)(2,1)S(1)} all-to-all(bf16[16,32,128]{2,1,0:T(8,128)(2,1)S(1)} %get-tuple-element.14), channel_id=1, replica_groups={{0,4,8,12,16,20,24,28,32,36,40,44,48,52,56,60},{64,68,72,76,80,84,88,92..., dimensions={0} | all-to-all | bytes 262144 | tf_op jit(solution)/shard_map/all_to_all | solution.py:458
  19.3 0.0 copy-done
  19.3 0.0 copy-done.1
  19.3 0.3 meet.1
  19.5 22.6 %all_to_all.27.refs_0_ = bf16[8,32,128]{2,1,0:T(8,128)(2,1)S(1)} all-to-all(bf16[8,32,128]{2,1,0:T(8,128)(2,1)S(1)} %get-tuple-element.15), channel_id=1, replica_groups={{0,64,128,192,256,320,384,448},{4,68,132,196,260,324,388,452},{8,72,136..., dimensions={0} | all-to-all | bytes 131072 | tf_op jit(solution)/shard_map/all_to_all | solution.py:471
  42.1 0.2 carry.1
  42.4 11.0 %all_to_all.28.back = bf16[16,24,128]{2,1,0:T(8,128)(2,1)S(1)} all-to-all(bf16[16,24,128]{2,1,0:T(8,128)(2,1)S(1)} %carry.1), channel_id=1, replica_groups={{0,4,8,12,16,20,24,28,32,36,40,44,48,52,56,60},{64,68,72,76,80,84,88,92..., dimensions={0} | all-to-all | bytes 196608 | tf_op jit(solution)/shard_map/all_to_all | solution.py:481
  53.4 1.1 %gate.1 = (f32[128,1024]{1,0:T(8,128)S(1)}, f32[4,128]{1,0:T(4,128)S(1)}) custom-call(bf16[16,24,128]{2,1,0:T(8,128)(2,1)S(1)} %all_to_all.28.back, f32[624,128]{1,0:T(8,128)S(1)} %get-tuple-element.17.kept, f32[120,8,128]{2,1,0:T(8,128)S(1)} %get-tuple-element.18.base, f32[120,8,128]{2,1,0:T(8,128)S(1)} %get-tuple-element.19.query, ...), custom_call_target="tpu_custom_call" | custom-call | tf_op jit(solution)/shard_map/gate/pallas_call | solution.py:483
  54.5 0.0 copy-start.2
  54.5 8.2 %all_to_all.29 = f32[4,1,128]{2,1,0:T(1,128)S(1)} all-to-all(f32[4,1,128]{2,1,0:T(1,128)S(1)} %bitcast.14), channel_id=1, replica_groups=mesh['ctx'=128,'tp'=4] {'tp'}, dimensions={0} | all-to-all | bytes 4096 | tf_op jit(solution)/shard_map/all_to_all | solution.py:501
  62.8 0.0 copy-done.2
  62.8 1.0 %norm.1 = bf16[128,1024]{1,0:T(8,128)(2,1)} custom-call(f32[128,1024]{1,0:T(8,128)S(1)} %get-tuple-element.21.refs_0_, f32[4,128]{1,0:T(4,128)S(1)} %bitcast.12, f32[1,1024]{1,0:T(1,128)S(1)} %bitcast.13), custom_call_target="tpu_custom_call" | custom-call | tf_op jit(solution)/shard_map/norm/pallas_call | solution.py:502
Async XLA Ops:
  3.6 15.7 %copy-start = (f32[3,7,1024]{2,1,0:T(8,128)S(1)}, f32[3,7,1024]{2,1,0:T(8,128)}, u32[]{:S(2)}) copy-start(f32[3,7,1024]{2,1,0:T(8,128)} %refs_4_.1) | copy-start | bytes 258052
  3.6 15.7 %copy-start.1 = (f32[1024,16]{0,1:T(8,128)S(1)}, f32[1024,16]{0,1:T(8,128)}, u32[]{:S(2)}) copy-start(f32[1024,16]{0,1:T(8,128)} %param.9) | copy-start | bytes 196612
  54.5 8.2 %copy-start.2 = (f32[1024]{0:T(1024)S(1)}, f32[1024]{0:T(1024)}, u32[]{:S(2)}) copy-start(f32[1024]{0:T(1024)} %param.11) | copy-start | bytes 12292

commit v4 on v3

--- a/solution.py
+++ b/solution.py
@@ -455,7 +455,9 @@
         compiler_params=on_chip(32),
     )(*(pltpu.with_memory_space_constraint(x, pltpu.HBM) for x in inputs))
 
+    message, spot = lax.optimization_barrier((message, lax.axis_index("ctx")))
     met = lax.all_to_all(message, "ctx", 0, 0, tiled=True, axis_index_groups=in_team)
+    met, spot = lax.optimization_barrier((met, spot))
     states, sent = pl.pallas_call(
         lambda *refs: meet_kernel(rows, length, teams, *refs),
         name="meet",
@@ -468,17 +470,31 @@
         scratch_shapes=[row_pair],
         compiler_params=on_chip(4),
     )(met, rate_t, short_taps)
+    def returned(from_teams):
+        back = pl.pallas_call(
+            lambda *refs: carry_kernel(rows, length, teams, *refs),
+            name="carry",
+            out_shape=jax.ShapeDtypeStruct((OWNERS, BACK, LANES), BF16),
+            in_specs=[whole()] * 5,
+            out_specs=whole(),
+            scratch_shapes=[row_pair, pltpu.VMEM((teams, 3 * HEAD, LANES), F32)],
+            compiler_params=on_chip(4),
+        )(from_teams, states, met, rate_t, short_taps)
+        return lax.all_to_all(back, "ctx", 0, 0, tiled=True, axis_index_groups=in_team)
+
+    first_team = spot < OWNERS
+    sent, ahead = lax.optimization_barrier(
+        (
+            sent,
+            lax.cond(
+                first_team,
+                lambda: returned(sent),
+                lambda: jnp.zeros((OWNERS, BACK, LANES), BF16),
+            ),
+        )
+    )
     gathered = lax.all_to_all(sent, "ctx", 0, 0, tiled=True, axis_index_groups=across)
-    back = pl.pallas_call(
-        lambda *refs: carry_kernel(rows, length, teams, *refs),
-        name="carry",
-        out_shape=jax.ShapeDtypeStruct((OWNERS, BACK, LANES), BF16),
-        in_specs=[whole()] * 5,
-        out_specs=whole(),
-        scratch_shapes=[row_pair, pltpu.VMEM((teams, 3 * HEAD, LANES), F32)],
-        compiler_params=on_chip(4),
-    )(gathered, states, met, rate_t, short_taps)
-    back = lax.all_to_all(back, "ctx", 0, 0, tiled=True, axis_index_groups=in_team)
+    back = lax.cond(first_team, lambda: ahead, lambda: returned(gathered))
 
     gated, squares = pl.pallas_call(
         gate_kernel,

time: 64.1 us -> 62.7 us (0.978)
  the two profiles are of different devices: /device:TPU:1 before, /device:TPU:64 now
where the time goes in v4:
time: 62.7 us; the launch traced here: 62.4 us
  blocking collectives  42.8 us (68%)
  Pallas kernels  6.88 us (11%)
  waiting for transfers between devices  6.7 us (11%)
  starting transfers between devices  5.9 us (9%)
    all_to_all x1, blocking collectives, shards(): lax.all_to_all(sent, 'ctx', 0, 0, tiled=True, axis_index_groups=across)  25.9 us
    all_to_all x1, blocking collectives, returned(): lax.all_to_all(back, 'ctx', 0, 0, tiled=True, axis_index_groups=in_team)  9 us
    all_to_all x1, blocking collectives, shards(): squares = lax.all_to_all(squares, 'tp', 0, 0, tiled=True)  7.88 us
    all_to_all x1, waiting for transfers between devices, shards(): lax.all_to_all(message, 'ctx', 0, 0, tiled=True, axis_index_groups=in_team)  6.7 us
    all_to_all x1, starting transfers between devices, shards(): lax.all_to_all(message, 'ctx', 0, 0, tiled=True, axis_index_groups=in_team)  5.9 us
    pallas_call x1, Pallas kernels, shards(): pl.pallas_call(lambda *refs: local_kernel(length, *refs), name='local', o...  4.26 us
  transfers between devices with their start and end apart: 1, of which 1 were waited for; matrix products, arithmetic and copies ran while one was open for 0% of the time, Pallas kernels for 0%

profile of v4, /device:TPU:64, one launch (start us, length us, event | category | flops | bytes accessed | tf_op | source)
XLA Modules:
  0.0 62.4 jit_solution(454755678070802129)
XLA Ops:
  0.0 4.3 %local.1 = (bf16[16,32,128]{2,1,0:T(8,128)(2,1)}, f32[120,8,128]{2,1,0:T(8,128)S(1)}, f32[120,8,128]{2,1,0:T(8,128)S(1)}, f32[624,128]{1,0:T(8,128)S(1)}, bf16[128,1024]{1,0:T(8,128)(2,1)S(1)}) custom-call(bf16[3,128,1024]{2,1,0:T(8,128)(2,1)} %bitcast.16, f32[3,7,1024]{2,1,0:T(8,128)} %refs_2_.1, f32[16,1024]{1,0:T(8,128)} %bitcast.12, ...), custom_call_target="tpu_custom_call" | custom-call | tf_op jit(solution)/shard_map/local/pallas_call | solution.py:435
  4.3 0.0 copy-start.1
  4.3 0.0 copy-start.2
  4.3 5.9 %all-to-all-start.2 = ((bf16[16,32,128]{2,1,0:T(8,128)(2,1)}), bf16[16,32,128]{2,1,0:T(8,128)(2,1)S(1)}, u32[]{:S(2)}, u32[]{:S(2)}) async-start(bf16[16,32,128]{2,1,0:T(8,128)(2,1)} %get-tuple-element.58), calls=%async_computation.2 | async-start | bytes 262144 | tf_op jit(solution)/shard_map/all_to_all | solution.py:459
  10.2 6.7 %all-to-all-done.2.refs_0_ = bf16[16,32,128]{2,1,0:T(8,128)(2,1)S(1)} async-done(((bf16[16,32,128]{2,1,0:T(8,128)(2,1)}), bf16[16,32,128]{2,1,0:T(8,128)(2,1)S(1)}, u32[]{:S(2)}, u32[]{:S(2)}) %all-to-all-start.2) | async-done | bytes 131104 | tf_op jit(solution)/shard_map/all_to_all | solution.py:459
  16.9 0.0 copy-done.1
  16.9 0.0 copy-done.2
  16.9 0.3 meet.1
  17.2 25.9 %all_to_all.31 = bf16[8,32,128]{2,1,0:T(8,128)(2,1)S(1)} all-to-all(bf16[8,32,128]{2,1,0:T(8,128)(2,1)S(1)} %get-tuple-element.64), channel_id=1, replica_groups={{0,64,128,192,256,320,384,448},{4,68,132,196,260,324,388,452},{8,72,136..., dimensions={0} | all-to-all | bytes 131072 | tf_op jit(solution)/shard_map/all_to_all | solution.py:496
  43.1 9.3 %conditional.3 = (bf16[16,24,128]{2,1,0:T(8,128)(2,1)S(1)}) conditional(s32[]{:T(128)} %convert_element_type.4, (bf16[8,32,128]{2,1,0:T(8,128)(2,1)S(1)}, f32[16,8,128]{2,1,0:T(8,128)S(1)}, bf16[16,32,128]{2,1,0:T(8,128)(2,1)S(1)}, f32[16,1024]{1,0:T(8,128)S(1)}, f32[3,7,1024]{2,1,0:T(8,128)S(1)}) %tuple.33, ...), branch_computations={%region_2.0_spmd, %region_3.0_spmd} | conditional | bytes 196616 | solution.py:497
  43.1 0.2 carry.3
  43.4 9.0 %all_to_all.30 = bf16[16,24,128]{2,1,0:T(8,128)(2,1)S(1)} all-to-all(bf16[16,24,128]{2,1,0:T(8,128)(2,1)S(1)} %carry.3), channel_id=1, replica_groups={{0,4,8,12,16,20,24,28,32,36,40,44,48,52,56,60},{64,68,72,76,80,84,88,92..., dimensions={0} | all-to-all | bytes 196608 | tf_op jit(solution)/shard_map/cond/branch_0_fun/all_to_all | solution.py:483
  52.4 1.1 %gate.1 = (f32[128,1024]{1,0:T(8,128)S(1)}, f32[4,128]{1,0:T(4,128)S(1)}) custom-call(bf16[16,24,128]{2,1,0:T(8,128)(2,1)S(1)} %get-tuple-element.73.back, f32[624,128]{1,0:T(8,128)S(1)} %get-tuple-element.66.kept, f32[120,8,128]{2,1,0:T(8,128)S(1)} %get-tuple-element.67.base, f32[120,8,128]{2,1,0:T(8,128)S(1)} %get-tuple-element.68.query, ...), custom_call_target="tpu_custom_call" | custom-call | tf_op jit(solution)/shard_map/gate/pallas_call | solution.py:499
  53.5 0.0 copy-start
  53.5 7.9 %all_to_all.32 = f32[4,1,128]{2,1,0:T(1,128)S(1)} all-to-all(f32[4,1,128]{2,1,0:T(1,128)S(1)} %bitcast.11), channel_id=1, replica_groups=mesh['ctx'=128,'tp'=4] {'tp'}, dimensions={0} | all-to-all | bytes 4096 | tf_op jit(solution)/shard_map/all_to_all | solution.py:517
  61.4 0.0 copy-done
  61.4 1.0 %norm.1 = bf16[128,1024]{1,0:T(8,128)(2,1)} custom-call(f32[128,1024]{1,0:T(8,128)S(1)} %get-tuple-element.70.refs_0_, f32[4,128]{1,0:T(4,128)S(1)} %bitcast.9, f32[1,1024]{1,0:T(1,128)S(1)} %bitcast.10), custom_call_target="tpu_custom_call" | custom-call | tf_op jit(solution)/shard_map/norm/pallas_call | solution.py:518
  (2 shorter events, 0.1 us)
Async XLA Ops:
  4.3 12.6 %copy-start.1 = (f32[3,7,1024]{2,1,0:T(8,128)S(1)}, f32[3,7,1024]{2,1,0:T(8,128)}, u32[]{:S(2)}) copy-start(f32[3,7,1024]{2,1,0:T(8,128)} %refs_2_.1) | copy-start | bytes 258052
  4.3 12.6 %copy-start.2 = (f32[1024,16]{0,1:T(8,128)S(1)}, f32[1024,16]{0,1:T(8,128)}, u32[]{:S(2)}) copy-start(f32[1024,16]{0,1:T(8,128)} %param.13) | copy-start | bytes 196612
  4.3 12.6 %all-to-all-start.2 = ((bf16[16,32,128]{2,1,0:T(8,128)(2,1)}), bf16[16,32,128]{2,1,0:T(8,128)(2,1)S(1)}, u32[]{:S(2)}, u32[]{:S(2)}) async-start(bf16[16,32,128]{2,1,0:T(8,128)(2,1)} %get-tuple-element.58), calls=%async_computation.2 | async-start | bytes 262144 | tf_op jit(solution)/shard_map/all_to_all | solution.py:459
  53.5 7.9 %copy-start = (f32[1024]{0:T(1024)S(1)}, f32[1024]{0:T(1024)}, u32[]{:S(2)}) copy-start(f32[1024]{0:T(1024)} %param.15) | copy-start | bytes 12292

commit v5 on v4

--- a/solution.py
+++ b/solution.py
@@ -455,22 +455,25 @@
         compiler_params=on_chip(32),
     )(*(pltpu.with_memory_space_constraint(x, pltpu.HBM) for x in inputs))
 
-    message, spot = lax.optimization_barrier((message, lax.axis_index("ctx")))
-    met = lax.all_to_all(message, "ctx", 0, 0, tiled=True, axis_index_groups=in_team)
-    met, spot = lax.optimization_barrier((met, spot))
-    states, sent = pl.pallas_call(
-        lambda *refs: meet_kernel(rows, length, teams, *refs),
-        name="meet",
-        out_shape=(
-            array(OWNERS, SUB, LANES),
-            jax.ShapeDtypeStruct((teams, 4 * HEAD, LANES), BF16),
-        ),
-        in_specs=[whole()] * 3,
-        out_specs=(whole(),) * 2,
-        scratch_shapes=[row_pair],
-        compiler_params=on_chip(4),
-    )(met, rate_t, short_taps)
-    def returned(from_teams):
+    def exchanged():
+        return lax.all_to_all(message, "ctx", 0, 0, tiled=True, axis_index_groups=in_team)
+
+    def combined(met):
+        states, sent = pl.pallas_call(
+            lambda *refs: meet_kernel(rows, length, teams, *refs),
+            name="meet",
+            out_shape=(
+                array(OWNERS, SUB, LANES),
+                jax.ShapeDtypeStruct((teams, 4 * HEAD, LANES), BF16),
+            ),
+            in_specs=[whole()] * 3,
+            out_specs=(whole(),) * 2,
+            scratch_shapes=[row_pair],
+            compiler_params=on_chip(4),
+        )(met, rate_t, short_taps)
+        return sent, states, met
+
+    def returned(from_teams, states, met):
         back = pl.pallas_call(
             lambda *refs: carry_kernel(rows, length, teams, *refs),
             name="carry",
@@ -482,19 +485,18 @@
         )(from_teams, states, met, rate_t, short_taps)
         return lax.all_to_all(back, "ctx", 0, 0, tiled=True, axis_index_groups=in_team)
 
-    first_team = spot < OWNERS
-    sent, ahead = lax.optimization_barrier(
-        (
-            sent,
-            lax.cond(
-                first_team,
-                lambda: returned(sent),
-                lambda: jnp.zeros((OWNERS, BACK, LANES), BF16),
-            ),
-        )
-    )
+    def first_round():
+        met = exchanged()
+        return met, returned(*combined(met))
+
+    def other_round():
+        return exchanged(), jnp.zeros((OWNERS, BACK, LANES), BF16)
+
+    first_team = lax.axis_index("ctx") < OWNERS
+    met, ahead = lax.cond(first_team, first_round, other_round)
+    sent, states, met = combined(met)
     gathered = lax.all_to_all(sent, "ctx", 0, 0, tiled=True, axis_index_groups=across)
-    back = lax.cond(first_team, lambda: ahead, lambda: returned(gathered))
+    back = lax.cond(first_team, lambda: ahead, lambda: returned(gathered, states, met))
 
     gated, squares = pl.pallas_call(
         gate_kernel,

time: 62.7 us -> 61.7 us (0.984)
  blocking collectives: 42.8 us -> 55.1 us
  waiting for transfers between devices: 6.7 us -> 0 us
  starting transfers between devices: 5.9 us -> 0 us
    all_to_all x0 -> x1, blocking collectives: none -> 12.3 us  [exchanged(): lax.all_to_all(message, 'ctx', 0, 0, tiled=True, axis_index_groups=in_team)]
    all_to_all x1 -> x0, waiting for transfers between devices: 6.7 us -> none  [shards(): lax.all_to_all(message, 'ctx', 0, 0, tiled=True, axis_index_groups=in_team)]
    all_to_all x1 -> x0, starting transfers between devices: 5.9 us -> none  [shards(): lax.all_to_all(message, 'ctx', 0, 0, tiled=True, axis_index_groups=in_team)]
  transfers between devices with their start and end apart: 1 -> 0, of which waited for: 1 -> 0; matrix products, arithmetic and copies ran while one was open for 0% -> 0% of each run, Pallas kernels for 0% -> 0%
where the time goes in v5:
time: 61.7 us; the launch traced here: 61.4 us
  blocking collectives  55.1 us (89%)
  Pallas kernels  6.27 us (10%)
    all_to_all x1, blocking collectives, shards(): lax.all_to_all(sent, 'ctx', 0, 0, tiled=True, axis_index_groups=across)  26 us
    all_to_all x1, blocking collectives, exchanged(): lax.all_to_all(message, 'ctx', 0, 0, tiled=True, axis_index_groups=in_team)  12.3 us
    all_to_all x1, blocking collectives, returned(): lax.all_to_all(back, 'ctx', 0, 0, tiled=True, axis_index_groups=in_team)  9 us
    all_to_all x1, blocking collectives, shards(): squares = lax.all_to_all(squares, 'tp', 0, 0, tiled=True)  7.77 us
    pallas_call x1, Pallas kernels, shards(): pl.pallas_call(lambda *refs: local_kernel(length, *refs), name='local', o...  3.64 us

profile of v5, /device:TPU:64, one launch (start us, length us, event | category | flops | bytes accessed | tf_op | source)
XLA Modules:
  0.0 61.4 jit_solution(3462722276207503352)
XLA Ops:
  0.0 0.0 copy-start.3
  0.0 0.0 copy-start.4
  0.0 3.6 %local.1 = (bf16[16,32,128]{2,1,0:T(8,128)(2,1)S(1)}, f32[120,8,128]{2,1,0:T(8,128)S(1)}, f32[120,8,128]{2,1,0:T(8,128)S(1)}, f32[624,128]{1,0:T(8,128)S(1)}, bf16[128,1024]{1,0:T(8,128)(2,1)S(1)}) custom-call(bf16[3,128,1024]{2,1,0:T(8,128)(2,1)} %bitcast.16, f32[3,7,1024]{2,1,0:T(8,128)} %refs_2_.1, f32[16,1024]{1,0:T(8,128)} %bitcast.12, ...), custom_call_target="tpu_custom_call" | custom-call | tf_op jit(solution)/shard_map/local/pallas_call | solution.py:435
  3.7 0.0 copy-done.3
  3.7 0.0 copy-done.4
  3.7 12.3 %conditional.2 = (bf16[16,32,128]{2,1,0:T(8,128)(2,1)S(1)}, bf16[16,24,128]{2,1,0:T(8,128)(2,1)S(1)}) conditional(s32[]{:T(128)} %convert_element_type.4, bf16[16,32,128]{2,1,0:T(8,128)(2,1)S(1)} %get-tuple-element.48, (bf16[16,32,128]{2,1,0:T(8,128)(2,1)S(1)}, f32[16,1024]{1,0:T(8,128)S(1)}, f32[3,7,1024]{2,1,0:T(8,128)S(1)}) %tuple.31), branch_computations={%region_0.0_spmd, %region_1.0_spmd} | conditional | bytes 1507400 | solution.py:496
  3.7 12.3 %all_to_all.32 = bf16[16,32,128]{2,1,0:T(8,128)(2,1)S(1)} all-to-all(bf16[16,32,128]{2,1,0:T(8,128)(2,1)S(1)} %param), channel_id=1, replica_groups={{0,4,8,12,16,20,24,28,32,36,40,44,48,52,56,60},{64,68,72,76,80,84,88,92..., dimensions={0} | all-to-all | bytes 262144 | tf_op jit(solution)/shard_map/cond/branch_0_fun/all_to_all | solution.py:459
  16.0 0.3 meet.3
  16.2 26.0 %all_to_all.36 = bf16[8,32,128]{2,1,0:T(8,128)(2,1)S(1)} all-to-all(bf16[8,32,128]{2,1,0:T(8,128)(2,1)S(1)} %get-tuple-element.50), channel_id=1, replica_groups={{0,64,128,192,256,320,384,448},{4,68,132,196,260,324,388,452},{8,72,136..., dimensions={0} | all-to-all | bytes 131072 | tf_op jit(solution)/shard_map/all_to_all | solution.py:498
  42.3 9.3 %conditional.3 = (bf16[16,24,128]{2,1,0:T(8,128)(2,1)S(1)}) conditional(s32[]{:T(128)} %convert_element_type.4, (bf16[8,32,128]{2,1,0:T(8,128)(2,1)S(1)}, f32[16,8,128]{2,1,0:T(8,128)S(1)}, bf16[16,32,128]{2,1,0:T(8,128)(2,1)S(1)}, f32[16,1024]{1,0:T(8,128)S(1)}, f32[3,7,1024]{2,1,0:T(8,128)S(1)}) %tuple.32, ...), branch_computations={%region_2.0_spmd, %region_3.0_spmd} | conditional | bytes 196616 | solution.py:499
  42.3 0.2 carry.3
  42.5 9.0 %all_to_all.35 = bf16[16,24,128]{2,1,0:T(8,128)(2,1)S(1)} all-to-all(bf16[16,24,128]{2,1,0:T(8,128)(2,1)S(1)} %carry.3), channel_id=1, replica_groups={{0,4,8,12,16,20,24,28,32,36,40,44,48,52,56,60},{64,68,72,76,80,84,88,92..., dimensions={0} | all-to-all | bytes 196608 | tf_op jit(solution)/shard_map/cond/branch_0_fun/all_to_all | solution.py:486
  51.5 1.1 %gate.1 = (f32[128,1024]{1,0:T(8,128)S(1)}, f32[4,128]{1,0:T(4,128)S(1)}) custom-call(bf16[16,24,128]{2,1,0:T(8,128)(2,1)S(1)} %get-tuple-element.63.back, f32[624,128]{1,0:T(8,128)S(1)} %get-tuple-element.53.kept, f32[120,8,128]{2,1,0:T(8,128)S(1)} %get-tuple-element.54.base, f32[120,8,128]{2,1,0:T(8,128)S(1)} %get-tuple-element.55.query, ...), custom_call_target="tpu_custom_call" | custom-call | tf_op jit(solution)/shard_map/gate/pallas_call | solution.py:501
  52.6 0.0 copy-start
  52.6 7.8 %all_to_all.37 = f32[4,1,128]{2,1,0:T(1,128)S(1)} all-to-all(f32[4,1,128]{2,1,0:T(1,128)S(1)} %bitcast.11), channel_id=1, replica_groups=mesh['ctx'=128,'tp'=4] {'tp'}, dimensions={0} | all-to-all | bytes 4096 | tf_op jit(solution)/shard_map/all_to_all | solution.py:519
  60.4 0.0 copy-done
  60.4 1.0 %norm.1 = bf16[128,1024]{1,0:T(8,128)(2,1)} custom-call(f32[128,1024]{1,0:T(8,128)S(1)} %get-tuple-element.57.refs_0_, f32[4,128]{1,0:T(4,128)S(1)} %bitcast.9, f32[1,1024]{1,0:T(1,128)S(1)} %bitcast.10), custom_call_target="tpu_custom_call" | custom-call | tf_op jit(solution)/shard_map/norm/pallas_call | solution.py:520
  (1 shorter events, 0.0 us)
Async XLA Ops:
  0.0 3.7 %copy-start.3 = (f32[3,7,1024]{2,1,0:T(8,128)S(1)}, f32[3,7,1024]{2,1,0:T(8,128)}, u32[]{:S(2)}) copy-start(f32[3,7,1024]{2,1,0:T(8,128)} %refs_2_.1) | copy-start | bytes 258052
  0.0 3.7 %copy-start.4 = (f32[1024,16]{0,1:T(8,128)S(1)}, f32[1024,16]{0,1:T(8,128)}, u32[]{:S(2)}) copy-start(f32[1024,16]{0,1:T(8,128)} %param.13) | copy-start | bytes 196612
  52.6 7.8 %copy-start = (f32[1024]{0:T(1024)S(1)}, f32[1024]{0:T(1024)}, u32[]{:S(2)}) copy-start(f32[1024]{0:T(1024)} %param.15) | copy-start | bytes 12292

commit v6 on v5

--- a/solution.py
+++ b/solution.py
@@ -22,7 +22,7 @@
 WEIGHT_AT = DECAY_AT + MODES
 SKIP_AT = WEIGHT_AT + MODES
 KEPT = SKIP_AT + 1
-EARLY = 2
+EARLY = 1
 HIGHEST = lax.Precision.HIGHEST
 F32 = jnp.float32
 BF16 = jnp.bfloat16
@@ -100,7 +100,7 @@
 
 
 def is_early():
-    return lax.axis_index("ctx") < EARLY * OWNERS
+    return lax.div(lax.axis_index("ctx"), OWNERS) == EARLY
 
 
 def local_kernel(
@@ -175,11 +175,11 @@
 
         def step_fn(step, state):
             if early:
-                return scan(step * 4, 4, decay, weight, direct, state, base_out, base_out)
-            return advance(step * 4, 4, decay, state, base_out)
+                return scan(step * 8, 8, decay, weight, direct, state, base_out, base_out)
+            return advance(step * 8, 8, decay, state, base_out)
 
         lax.fori_loop(0, (rows - HEAD) // GROUP, conv, 0)
-        state = lax.fori_loop(0, (rows - HEAD) // 4, step_fn, nothing())
+        state = lax.fori_loop(0, (rows - HEAD) // 8, step_fn, nothing())
         for n in range(MODES):
             state_s[n] = state[n]
 
@@ -342,22 +342,21 @@
         for value, m in zip(received(n), (n, n + SUB)):
             state[m] = decay[m] * weight[m] * value
 
-    def four(first, base, query, at, state):
-        for i in range(4):
+    def eight(first, base, query, at, state):
+        for i in range(8):
             value = query[first + i] * (base[first + i] + tree_sum(list(state)))
             tiles[pl.ds(pl.multiple_of((at + i) * SUB, SUB), SUB), :] = value
             state = [decay[n] * state[n] for n in range(MODES)]
         return tuple(state)
 
-    for at in range(0, HEAD, 4):
-        state = four(at, base_head, query_head, at, state)
+    state = eight(0, base_head, query_head, 0, state)
     state = tuple(state[n] + decay[n] * weight[n] * entered[n] for n in range(MODES))
 
     def apply(base, query):
         lax.fori_loop(
             0,
-            rest // 4,
-            lambda step, held: four(step * 4, base, query, step * 4 + HEAD, held),
+            rest // 8,
+            lambda step, held: eight(step * 8, base, query, step * 8 + HEAD, held),
             state,
         )
 

time: 61.7 us -> 61.6 us (level)
    all_to_all x1, blocking collectives: 7.77 us -> 8.68 us  [shards(): squares = lax.all_to_all(squares, 'tp', 0, 0, tiled=True)]
    all_to_all x1, blocking collectives: 26 us -> 25.2 us  [shards(): lax.all_to_all(sent, 'ctx', 0, 0, tiled=True, axis_index_groups=across)]
where the time goes in v6:
time: 61.6 us; the launch traced here: 61.3 us
  blocking collectives  55.1 us (89%)
  Pallas kernels  6.13 us (10%)
    all_to_all x1, blocking collectives, shards(): lax.all_to_all(sent, 'ctx', 0, 0, tiled=True, axis_index_groups=across)  25.2 us
    all_to_all x1, blocking collectives, exchanged(): lax.all_to_all(message, 'ctx', 0, 0, tiled=True, axis_index_groups=in_team)  12.3 us
    all_to_all x1, blocking collectives, returned(): lax.all_to_all(back, 'ctx', 0, 0, tiled=True, axis_index_groups=in_team)  9 us
    all_to_all x1, blocking collectives, shards(): squares = lax.all_to_all(squares, 'tp', 0, 0, tiled=True)  8.68 us
    pallas_call x1, Pallas kernels, shards(): pl.pallas_call(lambda *refs: local_kernel(length, *refs), name='local', o...  3.55 us

profile of v6, /device:TPU:64, one launch (start us, length us, event | category | flops | bytes accessed | tf_op | source)
XLA Modules:
  0.0 61.3 jit_solution(18337757691776310802)
XLA Ops:
  0.0 0.0 copy-start.3
  0.0 0.0 copy-start.4
  0.0 3.5 %local.1 = (bf16[16,32,128]{2,1,0:T(8,128)(2,1)S(1)}, f32[120,8,128]{2,1,0:T(8,128)S(1)}, f32[120,8,128]{2,1,0:T(8,128)S(1)}, f32[624,128]{1,0:T(8,128)S(1)}, bf16[128,1024]{1,0:T(8,128)(2,1)S(1)}) custom-call(bf16[3,128,1024]{2,1,0:T(8,128)(2,1)} %bitcast.16, f32[3,7,1024]{2,1,0:T(8,128)} %refs_2_.1, f32[16,1024]{1,0:T(8,128)} %bitcast.12, ...), custom_call_target="tpu_custom_call" | custom-call | tf_op jit(solution)/shard_map/local/pallas_call | solution.py:434
  3.6 0.0 copy-done.3
  3.6 0.0 copy-done.4
  3.6 12.3 %conditional.2 = (bf16[16,32,128]{2,1,0:T(8,128)(2,1)S(1)}, bf16[16,24,128]{2,1,0:T(8,128)(2,1)S(1)}) conditional(s32[]{:T(128)} %convert_element_type.4, bf16[16,32,128]{2,1,0:T(8,128)(2,1)S(1)} %get-tuple-element.48, (bf16[16,32,128]{2,1,0:T(8,128)(2,1)S(1)}, f32[16,1024]{1,0:T(8,128)S(1)}, f32[3,7,1024]{2,1,0:T(8,128)S(1)}) %tuple.31), branch_computations={%region_0.0_spmd, %region_1.0_spmd} | conditional | bytes 1507400 | solution.py:495
  3.6 12.3 %all_to_all.32 = bf16[16,32,128]{2,1,0:T(8,128)(2,1)S(1)} all-to-all(bf16[16,32,128]{2,1,0:T(8,128)(2,1)S(1)} %param), channel_id=1, replica_groups={{0,4,8,12,16,20,24,28,32,36,40,44,48,52,56,60},{64,68,72,76,80,84,88,92..., dimensions={0} | all-to-all | bytes 262144 | tf_op jit(solution)/shard_map/cond/branch_0_fun/all_to_all | solution.py:458
  15.9 0.3 meet.3
  16.1 25.2 %all_to_all.36 = bf16[8,32,128]{2,1,0:T(8,128)(2,1)S(1)} all-to-all(bf16[8,32,128]{2,1,0:T(8,128)(2,1)S(1)} %get-tuple-element.50), channel_id=1, replica_groups={{0,64,128,192,256,320,384,448},{4,68,132,196,260,324,388,452},{8,72,136..., dimensions={0} | all-to-all | bytes 131072 | tf_op jit(solution)/shard_map/all_to_all | solution.py:497
  41.3 9.3 %conditional.3 = (bf16[16,24,128]{2,1,0:T(8,128)(2,1)S(1)}) conditional(s32[]{:T(128)} %convert_element_type.4, (bf16[8,32,128]{2,1,0:T(8,128)(2,1)S(1)}, f32[16,8,128]{2,1,0:T(8,128)S(1)}, bf16[16,32,128]{2,1,0:T(8,128)(2,1)S(1)}, f32[16,1024]{1,0:T(8,128)S(1)}, f32[3,7,1024]{2,1,0:T(8,128)S(1)}) %tuple.32, ...), branch_computations={%region_2.0_spmd, %region_3.0_spmd} | conditional | bytes 196616 | solution.py:498
  41.3 0.2 carry.3
  41.5 9.0 %all_to_all.35 = bf16[16,24,128]{2,1,0:T(8,128)(2,1)S(1)} all-to-all(bf16[16,24,128]{2,1,0:T(8,128)(2,1)S(1)} %carry.3), channel_id=1, replica_groups={{0,4,8,12,16,20,24,28,32,36,40,44,48,52,56,60},{64,68,72,76,80,84,88,92..., dimensions={0} | all-to-all | bytes 196608 | tf_op jit(solution)/shard_map/cond/branch_0_fun/all_to_all | solution.py:485
  50.5 1.1 %gate.1 = (f32[128,1024]{1,0:T(8,128)S(1)}, f32[4,128]{1,0:T(4,128)S(1)}) custom-call(bf16[16,24,128]{2,1,0:T(8,128)(2,1)S(1)} %get-tuple-element.63.back, f32[624,128]{1,0:T(8,128)S(1)} %get-tuple-element.53.kept, f32[120,8,128]{2,1,0:T(8,128)S(1)} %get-tuple-element.54.base, f32[120,8,128]{2,1,0:T(8,128)S(1)} %get-tuple-element.55.query, ...), custom_call_target="tpu_custom_call" | custom-call | tf_op jit(solution)/shard_map/gate/pallas_call | solution.py:500
  51.6 0.0 copy-start
  51.6 8.7 %all_to_all.37 = f32[4,1,128]{2,1,0:T(1,128)S(1)} all-to-all(f32[4,1,128]{2,1,0:T(1,128)S(1)} %bitcast.11), channel_id=1, replica_groups=mesh['ctx'=128,'tp'=4] {'tp'}, dimensions={0} | all-to-all | bytes 4096 | tf_op jit(solution)/shard_map/all_to_all | solution.py:518
  60.3 0.0 copy-done
  60.3 1.0 %norm.1 = bf16[128,1024]{1,0:T(8,128)(2,1)} custom-call(f32[128,1024]{1,0:T(8,128)S(1)} %get-tuple-element.57.refs_0_, f32[4,128]{1,0:T(4,128)S(1)} %bitcast.9, f32[1,1024]{1,0:T(1,128)S(1)} %bitcast.10), custom_call_target="tpu_custom_call" | custom-call | tf_op jit(solution)/shard_map/norm/pallas_call | solution.py:519
  (1 shorter events, 0.0 us)
Async XLA Ops:
  0.0 3.6 %copy-start.3 = (f32[3,7,1024]{2,1,0:T(8,128)S(1)}, f32[3,7,1024]{2,1,0:T(8,128)}, u32[]{:S(2)}) copy-start(f32[3,7,1024]{2,1,0:T(8,128)} %refs_2_.1) | copy-start | bytes 258052
  0.0 3.6 %copy-start.4 = (f32[1024,16]{0,1:T(8,128)S(1)}, f32[1024,16]{0,1:T(8,128)}, u32[]{:S(2)}) copy-start(f32[1024,16]{0,1:T(8,128)} %param.13) | copy-start | bytes 196612
  51.6 8.7 %copy-start = (f32[1024]{0:T(1024)S(1)}, f32[1024]{0:T(1024)}, u32[]{:S(2)}) copy-start(f32[1024]{0:T(1024)} %param.15) | copy-start | bytes 12292

commit v7 on v6

--- a/solution.py
+++ b/solution.py
@@ -151,12 +151,6 @@
         spread(kept, TAP_AT + g * TAPS, taps[g], TAPS)
     spread(kept, DECAY_AT, jnp.exp(rates[...] * (-1.0 / length)), MODES)
     spread(kept, WEIGHT_AT, residues[...] * (1.0 / math.sqrt(length)), MODES)
-    copies[6].wait()
-    early = is_early()
-    spread(xs.at[0], 0, raw_out[:16].astype(F32), 16)
-    pl.when(early)(lambda: spread(xs.at[0], 0, raw_out[...].astype(F32), rows))
-    for g in range(3):
-        kept[pl.ds(g * HEAD * SUB, HEAD * SUB), :] = xs[g, : HEAD * SUB, :]
     decay, weight, direct = constants(kept)
 
     def conv_step(step, early):
@@ -183,8 +177,22 @@
         for n in range(MODES):
             state_s[n] = state[n]
 
-    pl.when(early)(lambda: finish(True))
-    pl.when(jnp.logical_not(early))(lambda: finish(False))
+    early = is_early()
+
+    @pl.when(early)
+    def _():
+        copies[6].wait()
+        spread(xs.at[0], 0, raw_out[...].astype(F32), rows)
+        finish(True)
+
+    @pl.when(jnp.logical_not(early))
+    def _():
+        finish(False)
+        copies[6].wait()
+        spread(xs.at[0], 0, raw_out[:16].astype(F32), 16)
+
+    for g in range(3):
+        kept[pl.ds(g * HEAD * SUB, HEAD * SUB), :] = xs[g, : HEAD * SUB, :]
 
     for n in range(SUB):
         for h, value in enumerate(paired(state_s[n], state_s[n + SUB])):

time: 61.6 us -> 61.6 us (level)
  no operation moved by 1% of the time
where the time goes in v7:
time: 61.6 us; the launch traced here: 61.3 us
  blocking collectives  55.1 us (89%)
  Pallas kernels  6.13 us (10%)
    all_to_all x1, blocking collectives, shards(): lax.all_to_all(sent, 'ctx', 0, 0, tiled=True, axis_index_groups=across)  25.1 us
    all_to_all x1, blocking collectives, exchanged(): lax.all_to_all(message, 'ctx', 0, 0, tiled=True, axis_index_groups=in_team)  12.3 us
    all_to_all x1, blocking collectives, returned(): lax.all_to_all(back, 'ctx', 0, 0, tiled=True, axis_index_groups=in_team)  9 us
    all_to_all x1, blocking collectives, shards(): squares = lax.all_to_all(squares, 'tp', 0, 0, tiled=True)  8.68 us
    pallas_call x1, Pallas kernels, shards(): pl.pallas_call(lambda *refs: local_kernel(length, *refs), name='local', o...  3.55 us

profile of v7, /device:TPU:64, one launch (start us, length us, event | category | flops | bytes accessed | tf_op | source)
XLA Modules:
  0.0 61.3 jit_solution(8758475354605635357)
XLA Ops:
  0.0 0.0 copy-start.3
  0.0 0.0 copy-start.4
  0.0 3.6 %local.1 = (bf16[16,32,128]{2,1,0:T(8,128)(2,1)S(1)}, f32[120,8,128]{2,1,0:T(8,128)S(1)}, f32[120,8,128]{2,1,0:T(8,128)S(1)}, f32[624,128]{1,0:T(8,128)S(1)}, bf16[128,1024]{1,0:T(8,128)(2,1)S(1)}) custom-call(bf16[3,128,1024]{2,1,0:T(8,128)(2,1)} %bitcast.16, f32[3,7,1024]{2,1,0:T(8,128)} %refs_2_.1, f32[16,1024]{1,0:T(8,128)} %bitcast.12, ...), custom_call_target="tpu_custom_call" | custom-call | tf_op jit(solution)/shard_map/local/pallas_call | solution.py:442
  3.6 0.0 copy-done.3
  3.6 0.0 copy-done.4
  3.6 12.3 %conditional.2 = (bf16[16,32,128]{2,1,0:T(8,128)(2,1)S(1)}, bf16[16,24,128]{2,1,0:T(8,128)(2,1)S(1)}) conditional(s32[]{:T(128)} %convert_element_type.4, bf16[16,32,128]{2,1,0:T(8,128)(2,1)S(1)} %get-tuple-element.48, (bf16[16,32,128]{2,1,0:T(8,128)(2,1)S(1)}, f32[16,1024]{1,0:T(8,128)S(1)}, f32[3,7,1024]{2,1,0:T(8,128)S(1)}) %tuple.31), branch_computations={%region_0.0_spmd, %region_1.0_spmd} | conditional | bytes 1507400 | solution.py:503
  3.6 12.3 %all_to_all.32 = bf16[16,32,128]{2,1,0:T(8,128)(2,1)S(1)} all-to-all(bf16[16,32,128]{2,1,0:T(8,128)(2,1)S(1)} %param), channel_id=1, replica_groups={{0,4,8,12,16,20,24,28,32,36,40,44,48,52,56,60},{64,68,72,76,80,84,88,92..., dimensions={0} | all-to-all | bytes 262144 | tf_op jit(solution)/shard_map/cond/branch_0_fun/all_to_all | solution.py:466
  15.9 0.3 meet.3
  16.1 25.1 %all_to_all.36 = bf16[8,32,128]{2,1,0:T(8,128)(2,1)S(1)} all-to-all(bf16[8,32,128]{2,1,0:T(8,128)(2,1)S(1)} %get-tuple-element.50), channel_id=1, replica_groups={{0,64,128,192,256,320,384,448},{4,68,132,196,260,324,388,452},{8,72,136..., dimensions={0} | all-to-all | bytes 131072 | tf_op jit(solution)/shard_map/all_to_all | solution.py:505
  41.3 9.3 %conditional.3 = (bf16[16,24,128]{2,1,0:T(8,128)(2,1)S(1)}) conditional(s32[]{:T(128)} %convert_element_type.4, (bf16[8,32,128]{2,1,0:T(8,128)(2,1)S(1)}, f32[16,8,128]{2,1,0:T(8,128)S(1)}, bf16[16,32,128]{2,1,0:T(8,128)(2,1)S(1)}, f32[16,1024]{1,0:T(8,128)S(1)}, f32[3,7,1024]{2,1,0:T(8,128)S(1)}) %tuple.32, ...), branch_computations={%region_2.0_spmd, %region_3.0_spmd} | conditional | bytes 196616 | solution.py:506
  41.3 0.2 carry.3
  41.5 9.0 %all_to_all.35 = bf16[16,24,128]{2,1,0:T(8,128)(2,1)S(1)} all-to-all(bf16[16,24,128]{2,1,0:T(8,128)(2,1)S(1)} %carry.3), channel_id=1, replica_groups={{0,4,8,12,16,20,24,28,32,36,40,44,48,52,56,60},{64,68,72,76,80,84,88,92..., dimensions={0} | all-to-all | bytes 196608 | tf_op jit(solution)/shard_map/cond/branch_0_fun/all_to_all | solution.py:493
  50.5 1.1 %gate.1 = (f32[128,1024]{1,0:T(8,128)S(1)}, f32[4,128]{1,0:T(4,128)S(1)}) custom-call(bf16[16,24,128]{2,1,0:T(8,128)(2,1)S(1)} %get-tuple-element.63.back, f32[624,128]{1,0:T(8,128)S(1)} %get-tuple-element.53.kept, f32[120,8,128]{2,1,0:T(8,128)S(1)} %get-tuple-element.54.base, f32[120,8,128]{2,1,0:T(8,128)S(1)} %get-tuple-element.55.query, ...), custom_call_target="tpu_custom_call" | custom-call | tf_op jit(solution)/shard_map/gate/pallas_call | solution.py:508
  51.6 0.0 copy-start
  51.6 8.7 %all_to_all.37 = f32[4,1,128]{2,1,0:T(1,128)S(1)} all-to-all(f32[4,1,128]{2,1,0:T(1,128)S(1)} %bitcast.11), channel_id=1, replica_groups=mesh['ctx'=128,'tp'=4] {'tp'}, dimensions={0} | all-to-all | bytes 4096 | tf_op jit(solution)/shard_map/all_to_all | solution.py:526
  60.3 0.0 copy-done
  60.3 1.0 %norm.1 = bf16[128,1024]{1,0:T(8,128)(2,1)} custom-call(f32[128,1024]{1,0:T(8,128)S(1)} %get-tuple-element.57.refs_0_, f32[4,128]{1,0:T(4,128)S(1)} %bitcast.9, f32[1,1024]{1,0:T(1,128)S(1)} %bitcast.10), custom_call_target="tpu_custom_call" | custom-call | tf_op jit(solution)/shard_map/norm/pallas_call | solution.py:527
  (1 shorter events, 0.0 us)
Async XLA Ops:
  0.0 3.6 %copy-start.3 = (f32[3,7,1024]{2,1,0:T(8,128)S(1)}, f32[3,7,1024]{2,1,0:T(8,128)}, u32[]{:S(2)}) copy-start(f32[3,7,1024]{2,1,0:T(8,128)} %refs_2_.1) | copy-start | bytes 258052
  0.0 3.6 %copy-start.4 = (f32[1024,16]{0,1:T(8,128)S(1)}, f32[1024,16]{0,1:T(8,128)}, u32[]{:S(2)}) copy-start(f32[1024,16]{0,1:T(8,128)} %param.13) | copy-start | bytes 196612
  51.6 8.7 %copy-start = (f32[1024]{0:T(1024)S(1)}, f32[1024]{0:T(1024)}, u32[]{:S(2)}) copy-start(f32[1024]{0:T(1024)} %param.15) | copy-start | bytes 12292

commit v8 on v6

--- a/solution.py
+++ b/solution.py
@@ -130,7 +130,7 @@
         (proj_hbm.at[0], raw_out),
     ]
     projections = (raw_out, proj.at[0], proj.at[1])
-    pieces[2:2] = [
+    pieces[:0] = [
         (taps_hbm, taps),
         (rates_hbm, rates),
         (residues_hbm, residues),
@@ -142,15 +142,15 @@
     for copy in copies:
         copy.start()
     rows = raw_out.shape[0]
-    for g, copy in ((1, copies[0]), (2, copies[1])):
-        copy.wait()
-        spread(xs.at[g], 0, projections[g][...].astype(F32), rows)
-    for copy in copies[2:6]:
+    for copy in copies[:4]:
         copy.wait()
     for g in range(3):
         spread(kept, TAP_AT + g * TAPS, taps[g], TAPS)
     spread(kept, DECAY_AT, jnp.exp(rates[...] * (-1.0 / length)), MODES)
     spread(kept, WEIGHT_AT, residues[...] * (1.0 / math.sqrt(length)), MODES)
+    for g, copy in ((1, copies[4]), (2, copies[5])):
+        copy.wait()
+        spread(xs.at[g], 0, projections[g][...].astype(F32), rows)
     copies[6].wait()
     early = is_early()
     spread(xs.at[0], 0, raw_out[:16].astype(F32), 16)

time: 61.6 us -> 61.7 us (level)
  no operation moved by 1% of the time
where the time goes in v8:
time: 61.7 us; the launch traced here: 61.4 us
  blocking collectives  55.1 us (89%)
  Pallas kernels  6.21 us (10%)
    all_to_all x1, blocking collectives, shards(): lax.all_to_all(sent, 'ctx', 0, 0, tiled=True, axis_index_groups=across)  25.2 us
    all_to_all x1, blocking collectives, exchanged(): lax.all_to_all(message, 'ctx', 0, 0, tiled=True, axis_index_groups=in_team)  12.3 us
    all_to_all x1, blocking collectives, returned(): lax.all_to_all(back, 'ctx', 0, 0, tiled=True, axis_index_groups=in_team)  9 us
    all_to_all x1, blocking collectives, shards(): squares = lax.all_to_all(squares, 'tp', 0, 0, tiled=True)  8.68 us
    pallas_call x1, Pallas kernels, shards(): pl.pallas_call(lambda *refs: local_kernel(length, *refs), name='local', o...  3.62 us

profile of v8, /device:TPU:64, one launch (start us, length us, event | category | flops | bytes accessed | tf_op | source)
XLA Modules:
  0.0 61.4 jit_solution(15788484257023477994)
XLA Ops:
  0.0 0.0 copy-start.3
  0.0 0.0 copy-start.4
  0.0 3.6 %local.1 = (bf16[16,32,128]{2,1,0:T(8,128)(2,1)S(1)}, f32[120,8,128]{2,1,0:T(8,128)S(1)}, f32[120,8,128]{2,1,0:T(8,128)S(1)}, f32[624,128]{1,0:T(8,128)S(1)}, bf16[128,1024]{1,0:T(8,128)(2,1)S(1)}) custom-call(bf16[3,128,1024]{2,1,0:T(8,128)(2,1)} %bitcast.16, f32[3,7,1024]{2,1,0:T(8,128)} %refs_2_.1, f32[16,1024]{1,0:T(8,128)} %bitcast.12, ...), custom_call_target="tpu_custom_call" | custom-call | tf_op jit(solution)/shard_map/local/pallas_call | solution.py:434
  3.6 0.0 copy-done.3
  3.6 0.0 copy-done.4
  3.7 12.3 %conditional.2 = (bf16[16,32,128]{2,1,0:T(8,128)(2,1)S(1)}, bf16[16,24,128]{2,1,0:T(8,128)(2,1)S(1)}) conditional(s32[]{:T(128)} %convert_element_type.4, bf16[16,32,128]{2,1,0:T(8,128)(2,1)S(1)} %get-tuple-element.48, (bf16[16,32,128]{2,1,0:T(8,128)(2,1)S(1)}, f32[16,1024]{1,0:T(8,128)S(1)}, f32[3,7,1024]{2,1,0:T(8,128)S(1)}) %tuple.31), branch_computations={%region_0.0_spmd, %region_1.0_spmd} | conditional | bytes 1507400 | solution.py:495
  3.7 12.3 %all_to_all.32 = bf16[16,32,128]{2,1,0:T(8,128)(2,1)S(1)} all-to-all(bf16[16,32,128]{2,1,0:T(8,128)(2,1)S(1)} %param), channel_id=1, replica_groups={{0,4,8,12,16,20,24,28,32,36,40,44,48,52,56,60},{64,68,72,76,80,84,88,92..., dimensions={0} | all-to-all | bytes 262144 | tf_op jit(solution)/shard_map/cond/branch_0_fun/all_to_all | solution.py:458
  16.0 0.3 meet.3
  16.2 25.2 %all_to_all.36 = bf16[8,32,128]{2,1,0:T(8,128)(2,1)S(1)} all-to-all(bf16[8,32,128]{2,1,0:T(8,128)(2,1)S(1)} %get-tuple-element.50), channel_id=1, replica_groups={{0,64,128,192,256,320,384,448},{4,68,132,196,260,324,388,452},{8,72,136..., dimensions={0} | all-to-all | bytes 131072 | tf_op jit(solution)/shard_map/all_to_all | solution.py:497
  41.4 9.3 %conditional.3 = (bf16[16,24,128]{2,1,0:T(8,128)(2,1)S(1)}) conditional(s32[]{:T(128)} %convert_element_type.4, (bf16[8,32,128]{2,1,0:T(8,128)(2,1)S(1)}, f32[16,8,128]{2,1,0:T(8,128)S(1)}, bf16[16,32,128]{2,1,0:T(8,128)(2,1)S(1)}, f32[16,1024]{1,0:T(8,128)S(1)}, f32[3,7,1024]{2,1,0:T(8,128)S(1)}) %tuple.32, ...), branch_computations={%region_2.0_spmd, %region_3.0_spmd} | conditional | bytes 196616 | solution.py:498
  41.4 0.2 carry.3
  41.6 9.0 %all_to_all.35 = bf16[16,24,128]{2,1,0:T(8,128)(2,1)S(1)} all-to-all(bf16[16,24,128]{2,1,0:T(8,128)(2,1)S(1)} %carry.3), channel_id=1, replica_groups={{0,4,8,12,16,20,24,28,32,36,40,44,48,52,56,60},{64,68,72,76,80,84,88,92..., dimensions={0} | all-to-all | bytes 196608 | tf_op jit(solution)/shard_map/cond/branch_0_fun/all_to_all | solution.py:485
  50.6 1.1 %gate.1 = (f32[128,1024]{1,0:T(8,128)S(1)}, f32[4,128]{1,0:T(4,128)S(1)}) custom-call(bf16[16,24,128]{2,1,0:T(8,128)(2,1)S(1)} %get-tuple-element.63.back, f32[624,128]{1,0:T(8,128)S(1)} %get-tuple-element.53.kept, f32[120,8,128]{2,1,0:T(8,128)S(1)} %get-tuple-element.54.base, f32[120,8,128]{2,1,0:T(8,128)S(1)} %get-tuple-element.55.query, ...), custom_call_target="tpu_custom_call" | custom-call | tf_op jit(solution)/shard_map/gate/pallas_call | solution.py:500
  51.7 0.0 copy-start
  51.7 8.7 %all_to_all.37 = f32[4,1,128]{2,1,0:T(1,128)S(1)} all-to-all(f32[4,1,128]{2,1,0:T(1,128)S(1)} %bitcast.11), channel_id=1, replica_groups=mesh['ctx'=128,'tp'=4] {'tp'}, dimensions={0} | all-to-all | bytes 4096 | tf_op jit(solution)/shard_map/all_to_all | solution.py:518
  60.4 0.0 copy-done
  60.4 1.0 %norm.1 = bf16[128,1024]{1,0:T(8,128)(2,1)} custom-call(f32[128,1024]{1,0:T(8,128)S(1)} %get-tuple-element.57.refs_0_, f32[4,128]{1,0:T(4,128)S(1)} %bitcast.9, f32[1,1024]{1,0:T(1,128)S(1)} %bitcast.10), custom_call_target="tpu_custom_call" | custom-call | tf_op jit(solution)/shard_map/norm/pallas_call | solution.py:519
  (1 shorter events, 0.0 us)
Async XLA Ops:
  0.0 3.6 %copy-start.3 = (f32[3,7,1024]{2,1,0:T(8,128)S(1)}, f32[3,7,1024]{2,1,0:T(8,128)}, u32[]{:S(2)}) copy-start(f32[3,7,1024]{2,1,0:T(8,128)} %refs_2_.1) | copy-start | bytes 258052
  0.0 3.6 %copy-start.4 = (f32[1024,16]{0,1:T(8,128)S(1)}, f32[1024,16]{0,1:T(8,128)}, u32[]{:S(2)}) copy-start(f32[1024,16]{0,1:T(8,128)} %param.13) | copy-start | bytes 196612
  51.7 8.7 %copy-start = (f32[1024]{0:T(1024)S(1)}, f32[1024]{0:T(1024)}, u32[]{:S(2)}) copy-start(f32[1024]{0:T(1024)} %param.15) | copy-start | bytes 12292
